TPU v7x, 128 devices: a whole 4x4x4 slice. The times are simulated.
128 devices in a mesh: dp: 4 (over y), sp: 32 (over z, x, core).
Axes of the slice: x: 4, y: 4, z: 4, core: 2. Of those that a mesh axis runs over, the one named last changes fastest.
Arguments:
- query_matrix: bfloat16 [4, 16384, 8192], P('dp', 'sp'), may hold values from -8 to 8
- key_matrix: bfloat16 [4, 16384, 1024], P('dp', 'sp'), may hold values from -8 to 8
- value_matrix: bfloat16 [4, 16384, 1024], P('dp', 'sp'), may hold values from -6 to 6
- block_source: int32 [32, 16], replicated, may hold values from 0 to 15, as said below
- documents: int32 [4, 128], P('dp'), may hold values from 0 to 31, never falling along the last dimension, each value on 1 to 8 neighbouring positions
Outputs:
- attended: bfloat16 [4, 16384, 8192], P('dp', 'sp')
Inputs may be any that keep to these rules, and one draw needn't show every extreme that they name: `block_source`: each row is a permutation of 0 to 15, and for every pair of dp indices g and h exactly 1 entries of row s at positions g * 4 to g * 4 + 3 lie in h * 4 to h * 4 + 3. `documents`: each row never falls, and a document spans at most 8 blocks.
All inputs are finite; a program needn't handle non-finite values.
Results may differ from a plain program's by a relative error of at most 0.0036.
Values may be sent and summed in bfloat16 or wider, within the bound.
A program may use at most 128 MiB of HBM per device.

v0:
```python
import jax
import jax.numpy as jnp
import numpy as np
from jax import lax
from jax.sharding import PartitionSpec as P

QUERY_HEADS = 64
KEY_VALUE_HEADS = 8
HEAD_WIDTH = 128
BALANCE_TOKENS = 128


def send_slots(dest_table, dp_index, block_list, capacity):
    is_mine = dest_table // block_list == dp_index
    order = jnp.argsort(jnp.where(is_mine, 0, 1), axis=1, stable=True)[:, :capacity]
    return (jnp.take_along_axis(dest_table, order, axis=1) % block_list).reshape(-1)


def arrival_index(sources, block_list, capacity):
    source_group = sources // block_list
    same_group = source_group[:, None] == source_group[None, :]
    earlier = jnp.arange(block_list)[None, :] < jnp.arange(block_list)[:, None]
    rank = jnp.sum(same_group & earlier, axis=1, dtype=jnp.int32)
    return source_group * capacity + rank


def attend(query_seq, key_seq, value_seq, block_docs):
    length = query_seq.shape[0]
    heads_dev = query_seq.shape[1]
    query_block = min(1024, length)
    key_block = query_block // 2
    query_count = length // query_block
    scale = HEAD_WIDTH ** (-0.5)
    token_docs = jnp.repeat(block_docs, BALANCE_TOKENS)
    doc_first = (
        jnp.sum(block_docs[None, :] < block_docs[:, None], axis=1, dtype=jnp.int32) * BALANCE_TOKENS
    )

    def one_block(block_number, output):
        start = block_number * query_block
        query_tile = lax.dynamic_slice_in_dim(query_seq, start, query_block, 0)
        query_docs = lax.dynamic_slice_in_dim(token_docs, start, query_block, 0)
        query_pos = start + jnp.arange(query_block, dtype=jnp.int32)
        first_tile = doc_first[start // BALANCE_TOKENS] // key_block
        end_tile = (start + query_block) // key_block

        def one_tile(tile_number, carry):
            top, total, summed = carry
            key_start = tile_number * key_block
            key_tile = lax.dynamic_slice_in_dim(key_seq, key_start, key_block, 0)
            value_tile = lax.dynamic_slice_in_dim(value_seq, key_start, key_block, 0)
            key_docs = lax.dynamic_slice_in_dim(token_docs, key_start, key_block, 0)
            key_pos = key_start + jnp.arange(key_block, dtype=jnp.int32)
            allowed = (query_docs[:, None] == key_docs[None, :]) & (
                key_pos[None, :] <= query_pos[:, None]
            )
            allowed = allowed[:, None, :]
            scores = (
                jnp.einsum("qhd,kd->qhk", query_tile, key_tile, preferred_element_type=jnp.float32)
                * scale
            )
            scores = jnp.where(allowed, scores, -1e30)
            new_top = jnp.maximum(top, jnp.max(scores, axis=-1))
            rescale = jnp.exp(top - new_top)
            weights = jnp.where(allowed, jnp.exp(scores - new_top[..., None]), 0.0)
            total = total * rescale + jnp.sum(weights, axis=-1)
            summed = summed * rescale[..., None] + jnp.einsum(
                "qhk,kd->qhd",
                weights.astype(jnp.bfloat16),
                value_tile,
                preferred_element_type=jnp.float32,
            )
            return (new_top, total, summed)

        start_carry = (
            jnp.full((query_block, heads_dev), -1e30, jnp.float32),
            jnp.zeros((query_block, heads_dev), jnp.float32),
            jnp.zeros((query_block, heads_dev, HEAD_WIDTH), jnp.float32),
        )
        top, total, summed = lax.fori_loop(first_tile, end_tile, one_tile, start_carry)
        result = (
            (summed / total[..., None])
            .astype(jnp.bfloat16)
            .reshape(query_block, heads_dev * HEAD_WIDTH)
        )
        return lax.dynamic_update_slice_in_dim(output, result, start, 0)

    empty = jnp.zeros((length, heads_dev * HEAD_WIDTH), jnp.bfloat16)
    return lax.fori_loop(0, query_count, one_block, empty)


def on_device(query_matrix, key_matrix, value_matrix, block_source, documents):
    dp_count = lax.axis_size("dp")
    sp_count = lax.axis_size("sp")
    dp_index = lax.axis_index("dp")
    sp_index = lax.axis_index("sp")
    tok_dev = query_matrix.shape[1]
    block_list = tok_dev // BALANCE_TOKENS
    capacity = block_list // dp_count
    heads_dev = QUERY_HEADS // sp_count
    group_length = QUERY_HEADS // KEY_VALUE_HEADS
    head_provider = np.array(
        [slot * heads_dev // group_length for slot in range(sp_count)], dtype=np.int32
    )
    routing = block_source.reshape(sp_count, dp_count, block_list)
    column_table = routing[sp_index]
    departing = send_slots(column_table, dp_index, block_list, capacity)
    local_q = query_matrix.reshape(block_list, BALANCE_TOKENS, QUERY_HEADS * HEAD_WIDTH)[departing]
    resident_keys = key_matrix.reshape(block_list, BALANCE_TOKENS, KEY_VALUE_HEADS * HEAD_WIDTH)[
        departing
    ]
    resident_values = value_matrix.reshape(
        block_list, BALANCE_TOKENS, KEY_VALUE_HEADS * HEAD_WIDTH
    )[departing]
    moved_q, shifted_keys, shifted_values = (
        lax.all_to_all(local_q, "dp", split_axis=0, concat_axis=0, tiled=True),
        lax.all_to_all(resident_keys, "dp", split_axis=0, concat_axis=0, tiled=True),
        lax.all_to_all(resident_values, "dp", split_axis=0, concat_axis=0, tiled=True),
    )
    arrival_order = arrival_index(column_table[dp_index], block_list, capacity)
    placed_q = moved_q[arrival_order].reshape(
        block_list, BALANCE_TOKENS, sp_count, heads_dev * HEAD_WIDTH
    )
    settled_keys = jnp.take(
        shifted_keys[arrival_order].reshape(
            block_list, BALANCE_TOKENS, KEY_VALUE_HEADS, HEAD_WIDTH
        ),
        head_provider,
        axis=2,
    )
    settled_values = jnp.take(
        shifted_values[arrival_order].reshape(
            block_list, BALANCE_TOKENS, KEY_VALUE_HEADS, HEAD_WIDTH
        ),
        head_provider,
        axis=2,
    )
    head_q, head_k, head_v = (
        lax.all_to_all(placed_q, "sp", split_axis=2, concat_axis=0, tiled=True),
        lax.all_to_all(settled_keys, "sp", split_axis=2, concat_axis=0, tiled=True),
        lax.all_to_all(settled_values, "sp", split_axis=2, concat_axis=0, tiled=True),
    )
    length = sp_count * tok_dev
    query_seq = head_q.reshape(length, heads_dev, HEAD_WIDTH)
    key_seq = head_k.reshape(length, HEAD_WIDTH)
    value_seq = head_v.reshape(length, HEAD_WIDTH)
    attended = attend(query_seq, key_seq, value_seq, documents[0])
    returned = lax.all_to_all(attended, "sp", split_axis=0, concat_axis=1, tiled=True)
    return returned.reshape(1, tok_dev, QUERY_HEADS * HEAD_WIDTH)


def solution(mesh):
    placed = (P("dp", "sp", None), P("dp", "sp", None), P("dp", "sp", None), P(), P("dp", None))
    return jax.shard_map(
        on_device, mesh=mesh, in_specs=placed, out_specs=P("dp", "sp", None), check_vma=False
    )
```

profile of v0, /device:TPU:0, one launch (start us, length us, event | category | flops | bytes accessed | tf_op | source)
XLA Modules:
  0.0 895.7 jit_solution(8268169604994503244)
XLA Ops:
  4.1 4.5 all-to-all-start.4
  10.3 6.0 fusion.33
  16.3 5.0 gather_fusion.5
  21.3 4.9 gather_fusion.6
  26.2 4.8 all-to-all-start.2
  31.0 7.9 pad_maximum_fusion
  38.9 6.7 all-to-all-done.2
  45.6 5.6 all-to-all-start
  55.9 3.0 gather_fusion.9
  58.9 84.6 %all-to-all-done = bf16[4,128,8192]{2,1,0:T(8,128)(2,1)} async-done(((bf16[4,128,8192]{2,1,0:T(8,128)(2,1)}), bf16[4,128,8192]{2,1,0:T(8,128)(2,1)}, u32[]{:S(2)}, u32[]{:S(2)}) %all-to-all-start) | async-done | bytes 8388640 | tf_op jit(solution)/shard_map/all_to_all | solution.py:116
  143.5 8.3 all-to-all-start.3
  151.8 6.0 fusion.32
  157.9 5.0 gather_fusion.7
  162.8 4.9 gather_fusion.8
  167.8 7.9 pad_maximum_fusion.1
  175.6 11.9 %copy.93 = bf16[4,128,8192]{1,2,0:T(8,128)(2,1)} copy(bf16[4,128,8192]{2,1,0:T(8,128)(2,1)} %pad_maximum_fusion.1) | data formatting | bytes 16777216
  187.6 7.9 copy.94
  195.4 9.8 %all-to-all-done.3 = bf16[4,128,32,128]{3,1,0,2:T(8,128)(2,1)} async-done(((bf16[4,128,32,128]{3,1,0,2:T(8,128)(2,1)}), bf16[4,128,32,128]{3,1,0,2:T(8,128)(2,1)}, u32[]{:S(2)}, u32[]{:S(2)}) %all-to-all-start.3) | async-done | bytes 4194336 | tf_op jit(solution)/shard_map/all_to_all | solution.py:140
  205.3 5.0 all-to-all-start.1
  212.2 3.0 gather_fusion.10
  215.3 100.9 %all-to-all-done.1 = bf16[4,128,32,256]{1,3,0,2:T(8,128)(2,1)} async-done(((bf16[4,128,32,256]{1,3,0,2:T(8,128)(2,1)}), bf16[4,128,32,256]{1,3,0,2:T(8,128)(2,1)}, u32[]{:S(2)}, u32[]{:S(2)}) %all-to-all-start.1) | async-done | bytes 8388640 | tf_op jit(solution)/shard_map/all_to_all | solution.py:139
  316.1 5.2 all-to-all-start.5
  321.5 11.9 %copy.95 = bf16[32,4,128,1,256]{4,2,1,0,3:T(8,128)(2,1)} copy(bf16[32,4,128,1,256]{2,4,1,0,3:T(8,128)(2,1)} %bitcast.17) | data formatting | bytes 16777216 | tf_op jit(solution)/shard_map/all_to_all | solution.py:139
  333.4 12.6 %reshape.268 = bf16[16384,2,128]{2,1,0:T(2,128)(2,1)} reshape(bf16[32,4,128,1,256]{4,2,1,0,3:T(8,128)(2,1)} %copy.95) | data formatting | bytes 16777216 | tf_op jit(solution)/shard_map/reshape | solution.py:144
  346.0 28.6 %all-to-all-done.5 = bf16[4,128,32,128]{3,1,0,2:T(8,128)(2,1)} async-done(((bf16[4,128,32,128]{3,1,0,2:T(8,128)(2,1)}), bf16[4,128,32,128]{3,1,0,2:T(8,128)(2,1)}, u32[]{:S(2)}, u32[]{:S(2)}) %all-to-all-start.5) | async-done | bytes 4194336 | tf_op jit(solution)/shard_map/all_to_all | solution.py:141
  374.6 3.6 broadcast_in_dim.44
  378.2 392.6 %while.64 = (s32[]{:T(128)}, bf16[16384,256]{1,0:T(8,128)(2,1)}, s32[128]{0:T(128)S(1)}, s32[16384]{0:T(1024)S(1)}, bf16[16384,2,128]{2,1,0:T(2,128)(2,1)}, /*in...) while((s32[]{:T(128)}, bf16[16384,256]{1,0:T(8,128)(2,1)}, ...), condition=%wide.region_8.10_spmd, body=%wide.region_3.9_spmd.sunk | while | flops 553129536 | bytes 22469708 | solution.py:89
  382.7 12.6 %while.65 = (s32[]{:T(128)}, f32[1024,2]{0,1:T(2,128)S(1)}, f32[1024,2]{0,1:T(2,128)S(1)}, f32[1024,2,128]{2,0,1:T(8,128)S(1)}, s32[]{:T(128)}, /*index=5*/s32[1...) while((s32[]{:T(128)}, f32[1024,2]{0,1:T(2,128)S(1)}, ...), condition=%wide.region_7.8_spmd.clone, body=%wide.region_4.7_spmd.clone.sunk | while | flops 552605184 | bytes 17717456 | solution.py:80
  400.9 18.9 %while.65 = (s32[]{:T(128)}, f32[1024,2]{0,1:T(2,128)S(1)}, f32[1024,2]{0,1:T(2,128)S(1)}, f32[1024,2,128]{2,0,1:T(8,128)S(1)}, s32[]{:T(128)}, /*index=5*/s32[1...) while((s32[]{:T(128)}, f32[1024,2]{0,1:T(2,128)S(1)}, ...), condition=%wide.region_7.8_spmd.clone, body=%wide.region_4.7_spmd.clone.sunk | while | flops 552605184 | bytes 17717456 | solution.py:80
  404.6 2.6 fusion.49
  410.9 2.6 fusion.49
  417.2 2.6 fusion.49
  425.4 18.9 %while.65 = (s32[]{:T(128)}, f32[1024,2]{0,1:T(2,128)S(1)}, f32[1024,2]{0,1:T(2,128)S(1)}, f32[1024,2,128]{2,0,1:T(8,128)S(1)}, s32[]{:T(128)}, /*index=5*/s32[1...) while((s32[]{:T(128)}, f32[1024,2]{0,1:T(2,128)S(1)}, ...), condition=%wide.region_7.8_spmd.clone, body=%wide.region_4.7_spmd.clone.sunk | while | flops 552605184 | bytes 17717456 | solution.py:80
  429.1 2.6 fusion.49
  435.4 2.6 fusion.49
  450.0 12.6 %while.65 = (s32[]{:T(128)}, f32[1024,2]{0,1:T(2,128)S(1)}, f32[1024,2]{0,1:T(2,128)S(1)}, f32[1024,2,128]{2,0,1:T(8,128)S(1)}, s32[]{:T(128)}, /*index=5*/s32[1...) while((s32[]{:T(128)}, f32[1024,2]{0,1:T(2,128)S(1)}, ...), condition=%wide.region_7.8_spmd.clone, body=%wide.region_4.7_spmd.clone.sunk | while | flops 552605184 | bytes 17717456 | solution.py:80
  453.7 2.6 fusion.49
  468.2 18.9 %while.65 = (s32[]{:T(128)}, f32[1024,2]{0,1:T(2,128)S(1)}, f32[1024,2]{0,1:T(2,128)S(1)}, f32[1024,2,128]{2,0,1:T(8,128)S(1)}, s32[]{:T(128)}, /*index=5*/s32[1...) while((s32[]{:T(128)}, f32[1024,2]{0,1:T(2,128)S(1)}, ...), condition=%wide.region_7.8_spmd.clone, body=%wide.region_4.7_spmd.clone.sunk | while | flops 552605184 | bytes 17717456 | solution.py:80
  471.9 2.6 fusion.49
  484.5 2.6 fusion.49
  492.7 18.9 %while.65 = (s32[]{:T(128)}, f32[1024,2]{0,1:T(2,128)S(1)}, f32[1024,2]{0,1:T(2,128)S(1)}, f32[1024,2,128]{2,0,1:T(8,128)S(1)}, s32[]{:T(128)}, /*index=5*/s32[1...) while((s32[]{:T(128)}, f32[1024,2]{0,1:T(2,128)S(1)}, ...), condition=%wide.region_7.8_spmd.clone, body=%wide.region_4.7_spmd.clone.sunk | while | flops 552605184 | bytes 17717456 | solution.py:80
  502.7 2.6 fusion.49
  517.3 18.9 %while.65 = (s32[]{:T(128)}, f32[1024,2]{0,1:T(2,128)S(1)}, f32[1024,2]{0,1:T(2,128)S(1)}, f32[1024,2,128]{2,0,1:T(8,128)S(1)}, s32[]{:T(128)}, /*index=5*/s32[1...) while((s32[]{:T(128)}, f32[1024,2]{0,1:T(2,128)S(1)}, ...), condition=%wide.region_7.8_spmd.clone, body=%wide.region_4.7_spmd.clone.sunk | while | flops 552605184 | bytes 17717456 | solution.py:80
  541.8 18.9 %while.65 = (s32[]{:T(128)}, f32[1024,2]{0,1:T(2,128)S(1)}, f32[1024,2]{0,1:T(2,128)S(1)}, f32[1024,2,128]{2,0,1:T(8,128)S(1)}, s32[]{:T(128)}, /*index=5*/s32[1...) while((s32[]{:T(128)}, f32[1024,2]{0,1:T(2,128)S(1)}, ...), condition=%wide.region_7.8_spmd.clone, body=%wide.region_4.7_spmd.clone.sunk | while | flops 552605184 | bytes 17717456 | solution.py:80
  558.1 2.6 fusion.49
  566.3 25.2 %while.65 = (s32[]{:T(128)}, f32[1024,2]{0,1:T(2,128)S(1)}, f32[1024,2]{0,1:T(2,128)S(1)}, f32[1024,2,128]{2,0,1:T(8,128)S(1)}, s32[]{:T(128)}, /*index=5*/s32[1...) while((s32[]{:T(128)}, f32[1024,2]{0,1:T(2,128)S(1)}, ...), condition=%wide.region_7.8_spmd.clone, body=%wide.region_4.7_spmd.clone.sunk | while | flops 552605184 | bytes 17717456 | solution.py:80
  576.4 2.6 fusion.49
  597.2 25.2 %while.65 = (s32[]{:T(128)}, f32[1024,2]{0,1:T(2,128)S(1)}, f32[1024,2]{0,1:T(2,128)S(1)}, f32[1024,2,128]{2,0,1:T(8,128)S(1)}, s32[]{:T(128)}, /*index=5*/s32[1...) while((s32[]{:T(128)}, f32[1024,2]{0,1:T(2,128)S(1)}, ...), condition=%wide.region_7.8_spmd.clone, body=%wide.region_4.7_spmd.clone.sunk | while | flops 552605184 | bytes 17717456 | solution.py:80
  628.0 25.2 %while.65 = (s32[]{:T(128)}, f32[1024,2]{0,1:T(2,128)S(1)}, f32[1024,2]{0,1:T(2,128)S(1)}, f32[1024,2,128]{2,0,1:T(8,128)S(1)}, s32[]{:T(128)}, /*index=5*/s32[1...) while((s32[]{:T(128)}, f32[1024,2]{0,1:T(2,128)S(1)}, ...), condition=%wide.region_7.8_spmd.clone, body=%wide.region_4.7_spmd.clone.sunk | while | flops 552605184 | bytes 17717456 | solution.py:80
  631.7 2.6 fusion.49
  644.4 2.6 fusion.49
  658.9 18.9 %while.65 = (s32[]{:T(128)}, f32[1024,2]{0,1:T(2,128)S(1)}, f32[1024,2]{0,1:T(2,128)S(1)}, f32[1024,2,128]{2,0,1:T(8,128)S(1)}, s32[]{:T(128)}, /*index=5*/s32[1...) while((s32[]{:T(128)}, f32[1024,2]{0,1:T(2,128)S(1)}, ...), condition=%wide.region_7.8_spmd.clone, body=%wide.region_4.7_spmd.clone.sunk | while | flops 552605184 | bytes 17717456 | solution.py:80
  662.6 2.6 fusion.49
  683.4 18.9 %while.65 = (s32[]{:T(128)}, f32[1024,2]{0,1:T(2,128)S(1)}, f32[1024,2]{0,1:T(2,128)S(1)}, f32[1024,2,128]{2,0,1:T(8,128)S(1)}, s32[]{:T(128)}, /*index=5*/s32[1...) while((s32[]{:T(128)}, f32[1024,2]{0,1:T(2,128)S(1)}, ...), condition=%wide.region_7.8_spmd.clone, body=%wide.region_4.7_spmd.clone.sunk | while | flops 552605184 | bytes 17717456 | solution.py:80
  699.7 2.6 fusion.49
  708.0 18.9 %while.65 = (s32[]{:T(128)}, f32[1024,2]{0,1:T(2,128)S(1)}, f32[1024,2]{0,1:T(2,128)S(1)}, f32[1024,2,128]{2,0,1:T(8,128)S(1)}, s32[]{:T(128)}, /*index=5*/s32[1...) while((s32[]{:T(128)}, f32[1024,2]{0,1:T(2,128)S(1)}, ...), condition=%wide.region_7.8_spmd.clone, body=%wide.region_4.7_spmd.clone.sunk | while | flops 552605184 | bytes 17717456 | solution.py:80
  718.0 2.6 fusion.49
  732.5 18.9 %while.65 = (s32[]{:T(128)}, f32[1024,2]{0,1:T(2,128)S(1)}, f32[1024,2]{0,1:T(2,128)S(1)}, f32[1024,2,128]{2,0,1:T(8,128)S(1)}, s32[]{:T(128)}, /*index=5*/s32[1...) while((s32[]{:T(128)}, f32[1024,2]{0,1:T(2,128)S(1)}, ...), condition=%wide.region_7.8_spmd.clone, body=%wide.region_4.7_spmd.clone.sunk | while | flops 552605184 | bytes 17717456 | solution.py:80
  736.2 2.6 fusion.49
  748.8 2.6 fusion.49
  757.0 12.6 %while.65 = (s32[]{:T(128)}, f32[1024,2]{0,1:T(2,128)S(1)}, f32[1024,2]{0,1:T(2,128)S(1)}, f32[1024,2,128]{2,0,1:T(8,128)S(1)}, s32[]{:T(128)}, /*index=5*/s32[1...) while((s32[]{:T(128)}, f32[1024,2]{0,1:T(2,128)S(1)}, ...), condition=%wide.region_7.8_spmd.clone, body=%wide.region_4.7_spmd.clone.sunk | while | flops 552605184 | bytes 17717456 | solution.py:80
  770.8 100.9 %all_to_all.76 = bf16[32,512,256]{2,1,0:T(8,128)(2,1)} all-to-all(bf16[32,512,256]{2,1,0:T(8,128)(2,1)} %bitcast.136), channel_id=1, replica_groups=mesh['dp'=4,'sp'=32] {'sp'}, dimensions={0} | all-to-all | bytes 16777216 | tf_op jit(solution)/shard_map/all_to_all | solution.py:148
  871.7 11.9 %copy.101 = bf16[32,512,256]{1,2,0:T(8,128)(2,1)} copy(bf16[32,512,256]{2,1,0:T(8,128)(2,1)} %all_to_all.76) | data formatting | bytes 16777216 | tf_op jit(solution)/shard_map/all_to_all | solution.py:148
  883.7 12.0 %copy.102 = bf16[1,512,8192]{2,1,0:T(8,128)(2,1)} copy(bf16[1,512,8192]{1,2,0:T(8,128)(2,1)} %bitcast.138) | data formatting | bytes 16777216 | tf_op jit(solution)/shard_map/reshape | solution.py:149
  (631 shorter events, 317.7 us)
Async XLA Ops:
  0.0 2.5 copy-start
  0.0 8.6 copy-start.2
  4.1 22.1 %all-to-all-start.4 = ((bf16[4,128,1024]{2,1,0:T(8,128)(2,1)}), bf16[4,128,1024]{2,1,0:T(8,128)(2,1)S(1)}, u32[]{:S(2)}, u32[]{:S(2)}) async-start(bf16[4,128,1024]{2,1,0:T(8,128)(2,1)} %gather_fusion.2), calls=%async_computation.4 | async-start | bytes 2097152 | tf_op jit(solution)/shard_map/all_to_all | solution.py:118
  26.2 19.3 %all-to-all-start.2 = ((bf16[4,128,1024]{2,1,0:T(8,128)(2,1)}), bf16[4,128,1024]{2,1,0:T(8,128)(2,1)S(1)}, u32[]{:S(2)}, u32[]{:S(2)}) async-start(bf16[4,128,1024]{2,1,0:T(8,128)(2,1)} %gather_fusion), calls=%async_computation.2 | async-start | bytes 2097152 | tf_op jit(solution)/shard_map/all_to_all | solution.py:117
  38.9 13.4 %copy-start.4 = (s32[32]{0:T(128)S(1)}, s32[32]{0:T(128)}, u32[]{:S(2)}) copy-start(s32[32]{0:T(128)} %constant.315) | copy-start | bytes 388
  45.6 98.0 %all-to-all-start = ((bf16[4,128,8192]{2,1,0:T(8,128)(2,1)}), bf16[4,128,8192]{2,1,0:T(8,128)(2,1)}, u32[]{:S(2)}, u32[]{:S(2)}) async-start(bf16[4,128,8192]{2,1,0:T(8,128)(2,1)} %pad_maximum_fusion), calls=%async_computation | async-start | bytes 16777216 | tf_op jit(solution)/shard_map/all_to_all | solution.py:116
  143.5 61.8 %all-to-all-start.3 = ((bf16[4,128,32,128]{3,1,0,2:T(8,128)(2,1)}), bf16[4,128,32,128]{3,1,0,2:T(8,128)(2,1)}, u32[]{:S(2)}, u32[]{:S(2)}) async-start(bf16[4,128,32,128]{3,1,0,2:T(8,128)(2,1)} %bitcast.139), calls=%async_computation.3 | async-start | bytes 8388608 | tf_op jit(solution)/shard_map/all_to_all | solution.py:140
  205.3 110.8 %all-to-all-start.1 = ((bf16[4,128,32,256]{1,3,0,2:T(8,128)(2,1)}), bf16[4,128,32,256]{1,3,0,2:T(8,128)(2,1)}, u32[]{:S(2)}, u32[]{:S(2)}) async-start(bf16[4,128,32,256]{1,3,0,2:T(8,128)(2,1)} %copy.94), calls=%async_computation.1 | async-start | bytes 16777216 | tf_op jit(solution)/shard_map/all_to_all | solution.py:139
  316.1 5.2 copy-start.3
  316.1 58.5 %all-to-all-start.5 = ((bf16[4,128,32,128]{3,1,0,2:T(8,128)(2,1)}), bf16[4,128,32,128]{3,1,0,2:T(8,128)(2,1)}, u32[]{:S(2)}, u32[]{:S(2)}) async-start(bf16[4,128,32,128]{3,1,0,2:T(8,128)(2,1)} %bitcast.140), calls=%async_computation.5 | async-start | bytes 8388608 | tf_op jit(solution)/shard_map/all_to_all | solution.py:141
  883.7 12.0 %copy-start.1 = (bf16[1,512,1024]{2,1,0:T(8,128)(2,1)S(1)}, bf16[1,512,1024]{2,1,0:T(8,128)(2,1)}, u32[]{:S(2)}) copy-start(bf16[1,512,1024]{2,1,0:T(8,128)(2,1)} %param.14) | copy-start | bytes 3145732
where the time goes:
time: 900 us; the launch traced here: 896 us
  waiting for transfers between devices  231 us (26%)
  matrix products  217 us (24%)
  local copies, waits for them, and re-layouts  159 us (18%)
  other arithmetic  113 us (13%)
  blocking collectives  101 us (11%)
  loops' own time  40.7 us (5%)
  starting transfers between devices  33.4 us (4%)
    dot_general x48, matrix products, one_tile(): jnp.einsum('qhk,kd->qhd', weights.astype(jnp.bfloat16), value_tile, prefe...  124 us
    all_to_all x1, blocking collectives, on_device(): lax.all_to_all(attended, 'sp', split_axis=0, concat_axis=1, tiled=True)  101 us
    all_to_all x1, waiting for transfers between devices, on_device(): lax.all_to_all(placed_q, 'sp', split_axis=2, concat_axis=0, tiled=True)  101 us
    dot_general x48, matrix products, one_tile(): jnp.einsum('qhd,kd->qhk', query_tile, key_tile, preferred_element_type=jn...  92.6 us
    all_to_all x1, waiting for transfers between devices, on_device(): lax.all_to_all(local_q, 'dp', split_axis=0, concat_axis=0, tiled=True)  84.6 us
    reduce_sum x48, other arithmetic, one_tile(): total = total * rescale + jnp.sum(weights, axis=-1)  53.2 us
    another operation x1, loops' own time, attend(): return lax.fori_loop(0, query_count, one_block, empty)  37.1 us
    all_to_all x1, waiting for transfers between devices, on_device(): lax.all_to_all(settled_values, 'sp', split_axis=2, concat_axis=0, tiled=T...  28.6 us
  transfers between devices with their start and end apart: 6, of which 5 were waited for; matrix products, arithmetic and copies ran while one was open for 12% of the time, Pallas kernels for 0%

commit v1 on v0

v1 whole, which is shorter than its diff:
```python
import jax
import jax.numpy as jnp
from jax import lax
from jax.experimental import pallas as pl
from jax.experimental.pallas import tpu as pltpu
from jax.sharding import PartitionSpec as P

QUERY_HEADS = 64
KEY_VALUE_HEADS = 8
HEAD_WIDTH = 128
BALANCE_TOKENS = 128
MOST_BLK = 8
BLK_DEV = 4
N_DP = 4
N_SP = 32
GROUP = QUERY_HEADS // KEY_VALUE_HEADS
CHUNKS = KEY_VALUE_HEADS
CHUNK_WIDTH = GROUP * HEAD_WIDTH
HALO = MOST_BLK - 1
WINDOW = HALO + BLK_DEV
SPAN = MOST_BLK * BALANCE_TOKENS
MASKED = -1e30
LOG2E = 1.4426950408889634
MESH = pl.DeviceIdType.MESH


def fused_kernel(
    source_ref,
    docs_ref,
    q_hbm,
    k_hbm,
    v_hbm,
    out_hbm,
    q_local,
    k_local,
    v_local,
    q_send,
    q_recv,
    kv_send,
    kv_recv,
    window,
    q_slots,
    bias,
    staged,
    load_sem,
    q_send_sem,
    q_recv_sem,
    kv_send_sem,
    kv_recv_sem,
    halo_send_sem,
    halo_recv_sem,
    store_sem,
):
    g = lax.axis_index("dp")
    s = lax.axis_index("sp")

    def dp_peer(step):
        return (lax.rem(g + step, N_DP), s)

    def sp_peer(step):
        return (g, lax.rem(s + step + N_SP, N_SP))

    k_load = pltpu.make_async_copy(k_hbm, k_local, load_sem.at[0])
    v_load = pltpu.make_async_copy(v_hbm, v_local, load_sem.at[1])

    def q_load(c):
        columns = pl.ds(pl.multiple_of(c * CHUNK_WIDTH, CHUNK_WIDTH), CHUNK_WIDTH)
        return pltpu.make_async_copy(q_hbm.at[:, :, columns], q_local.at[c], load_sem.at[2 + c])

    k_load.start()
    v_load.start()

    @pl.loop(0, CHUNKS)
    def _(c):
        q_load(c).start()

    barrier = pltpu.get_barrier_semaphore()
    for step in range(1, N_DP):
        pl.semaphore_signal(barrier, 1, device_id=dp_peer(step), device_id_type=MESH)
    for step in (1, 2, -1, -2):
        pl.semaphore_signal(barrier, 1, device_id=sp_peer(step), device_id_type=MESH)

    def departing(step):
        dest = lax.rem(g + step, N_DP)
        chosen = 0
        for slot in range(BLK_DEV):
            entry = source_ref[s, dest * BLK_DEV + slot]
            chosen = chosen + jnp.where((entry >> 2) == g, entry & 3, 0)
        return chosen

    def arrived_from(slot):
        entry = source_ref[s, g * BLK_DEV + slot]
        return (g - (entry >> 2)) & 3

    leaves = [departing(step) for step in range(N_DP)]
    comes = [arrived_from(slot) for slot in range(BLK_DEV)]

    for slot in range(BLK_DEV):
        own = docs_ref[s * BLK_DEV + slot]
        for j in range(HALO):
            block = s * BLK_DEV + slot + j - HALO
            same = (docs_ref[jnp.maximum(block, 0)] == own) & (block >= 0)
            level = jnp.where(same, 0.0, MASKED).astype(jnp.float32)
            bias[slot, :, pl.ds(j * BALANCE_TOKENS, BALANCE_TOKENS)] = jnp.full(
                (8, BALANCE_TOKENS), level, jnp.float32
            )

    def kv_copy(step):
        return pltpu.make_async_remote_copy(
            src_ref=kv_send.at[step - 1],
            dst_ref=kv_recv.at[step],
            send_sem=kv_send_sem.at[step - 1],
            recv_sem=kv_recv_sem.at[step - 1],
            device_id=dp_peer(step),
            device_id_type=MESH,
        )

    def q_copy(c, step):
        return pltpu.make_async_remote_copy(
            src_ref=q_send.at[c, step - 1],
            dst_ref=q_recv.at[c, step],
            send_sem=q_send_sem.at[c, step - 1],
            recv_sem=q_recv_sem.at[c, step - 1],
            device_id=dp_peer(step),
            device_id_type=MESH,
        )

    def near_copy(c):
        return pltpu.make_async_remote_copy(
            src_ref=window.at[c, pl.ds(HALO, BLK_DEV)],
            dst_ref=window.at[c, pl.ds(HALO - BLK_DEV, BLK_DEV)],
            send_sem=halo_send_sem.at[c, 0],
            recv_sem=halo_recv_sem.at[c, 0],
            device_id=sp_peer(1),
            device_id_type=MESH,
        )

    def far_copy(c):
        return pltpu.make_async_remote_copy(
            src_ref=window.at[c, pl.ds(WINDOW - (HALO - BLK_DEV), HALO - BLK_DEV)],
            dst_ref=window.at[c, pl.ds(0, HALO - BLK_DEV)],
            send_sem=halo_send_sem.at[c, 1],
            recv_sem=halo_recv_sem.at[c, 1],
            device_id=sp_peer(2),
            device_id_type=MESH,
        )

    k_load.wait()
    v_load.wait()
    for step in range(N_DP):
        target = kv_recv.at[0] if step == 0 else kv_send.at[step - 1]
        for c in range(CHUNKS):
            columns = pl.ds(c * HEAD_WIDTH, HEAD_WIDTH)
            target[c, 0] = k_local[leaves[step], :, columns]
            target[c, 1] = v_local[leaves[step], :, columns]

    pl.semaphore_wait(barrier, 7)
    for step in range(1, N_DP):
        kv_copy(step).start()

    @pl.loop(0, CHUNKS)
    def _(c):
        q_load(c).wait()

    @pl.loop(0, CHUNKS)
    def _(c):
        for step in range(1, N_DP):
            q_send[c, step - 1] = q_local[c, leaves[step]]
            q_copy(c, step).start()
        q_recv[c, 0] = q_local[c, leaves[0]]

    for step in range(1, N_DP):
        kv_copy(step).wait_recv()
    for slot in range(BLK_DEV):
        for c in range(CHUNKS):
            window[c, HALO + slot] = kv_recv[comes[slot], c]

    @pl.loop(0, CHUNKS)
    def _(c):
        near_copy(c).start()
        far_copy(c).start()

    row = lax.broadcasted_iota(jnp.int32, (BALANCE_TOKENS, BALANCE_TOKENS), 0)
    column = lax.broadcasted_iota(jnp.int32, (BALANCE_TOKENS, BALANCE_TOKENS), 1)
    triangle = jnp.where(column <= row, 0.0, MASKED).astype(jnp.float32)
    diagonal = jnp.concatenate([triangle, triangle], axis=0)
    factor = LOG2E * HEAD_WIDTH ** -0.5

    def store_copy(c):
        columns = pl.ds(pl.multiple_of(c * CHUNK_WIDTH, CHUNK_WIDTH), CHUNK_WIDTH)
        return pltpu.make_async_copy(
            staged.at[lax.rem(c, 2)], out_hbm.at[:, :, columns], store_sem.at[lax.rem(c, 2)]
        )

    @pl.loop(0, CHUNKS)
    def _(c):
        near_copy(c).wait_recv()
        far_copy(c).wait_recv()
        for step in range(1, N_DP):
            q_copy(c, step).wait_recv()

        @pl.when(c >= 2)
        def _():
            store_copy(c - 2).wait()

        for slot in range(BLK_DEV):
            for head in range(GROUP):
                columns = pl.ds(head * HEAD_WIDTH, HEAD_WIDTH)
                chosen = q_recv[c, 0, :, columns]
                for step in range(1, N_DP):
                    chosen = jnp.where(comes[slot] == step, q_recv[c, step, :, columns], chosen)
                q_slots[slot, pl.ds(head * BALANCE_TOKENS, BALANCE_TOKENS)] = chosen

        side = lax.rem(c, 2)

        @pl.loop(0, BLK_DEV)
        def _(slot):
            keys = window[c, pl.ds(slot, MOST_BLK), 0].reshape(SPAN, HEAD_WIDTH)
            values = window[c, pl.ds(slot, MOST_BLK), 1].reshape(SPAN, HEAD_WIDTH)
            level = bias[slot, pl.ds(0, 1)]
            for pair in range(GROUP // 2):
                queries = q_slots[slot, pl.ds(pair * 2 * BALANCE_TOKENS, 2 * BALANCE_TOKENS)]
                scores = lax.dot_general(
                    queries, keys, (((1,), (1,)), ((), ())), preferred_element_type=jnp.float32
                )
                far = scores[:, : HALO * BALANCE_TOKENS] + level
                near = scores[:, HALO * BALANCE_TOKENS :] + diagonal
                scores = jnp.concatenate([far, near], axis=1)
                top = jnp.max(scores, axis=1, keepdims=True)
                weights = jnp.exp2((scores - top) * factor)
                total = jnp.sum(weights, axis=1, keepdims=True)
                mixed = jnp.dot(
                    weights.astype(jnp.bfloat16), values, preferred_element_type=jnp.float32
                )
                result = (mixed / total).astype(jnp.bfloat16)
                for part in range(2):
                    staged[
                        side, slot, :, pl.ds((2 * pair + part) * HEAD_WIDTH, HEAD_WIDTH)
                    ] = result[part * BALANCE_TOKENS : (part + 1) * BALANCE_TOKENS]

        store_copy(c).start()

    store_copy(CHUNKS - 2).wait()
    store_copy(CHUNKS - 1).wait()
    for step in range(1, N_DP):
        kv_copy(step).wait_send()

    @pl.loop(0, CHUNKS)
    def _(c):
        near_copy(c).wait_send()
        far_copy(c).wait_send()
        for step in range(1, N_DP):
            q_copy(c, step).wait_send()


def on_device(query_matrix, key_matrix, value_matrix, block_source, documents):
    bf16 = jnp.bfloat16
    tokens = BALANCE_TOKENS
    blocks = (BLK_DEV, tokens)
    dma = pltpu.SemaphoreType.DMA
    kv_width = KEY_VALUE_HEADS * HEAD_WIDTH
    width = QUERY_HEADS * HEAD_WIDTH
    smem = pl.BlockSpec(memory_space=pltpu.SMEM)
    anywhere = pl.BlockSpec(memory_space=pl.ANY)
    attended = pl.pallas_call(
        fused_kernel,
        out_shape=jax.ShapeDtypeStruct((*blocks, width), bf16),
        in_specs=[smem, smem, anywhere, anywhere, anywhere],
        out_specs=anywhere,
        scratch_shapes=[
            pltpu.VMEM((CHUNKS, *blocks, CHUNK_WIDTH), bf16),
            pltpu.VMEM((*blocks, kv_width), bf16),
            pltpu.VMEM((*blocks, kv_width), bf16),
            pltpu.VMEM((CHUNKS, N_DP - 1, tokens, CHUNK_WIDTH), bf16),
            pltpu.VMEM((CHUNKS, N_DP, tokens, CHUNK_WIDTH), bf16),
            pltpu.VMEM((N_DP - 1, CHUNKS, 2, tokens, HEAD_WIDTH), bf16),
            pltpu.VMEM((N_DP, CHUNKS, 2, tokens, HEAD_WIDTH), bf16),
            pltpu.VMEM((CHUNKS, WINDOW, 2, tokens, HEAD_WIDTH), bf16),
            pltpu.VMEM((BLK_DEV, GROUP * tokens, HEAD_WIDTH), bf16),
            pltpu.VMEM((BLK_DEV, 8, HALO * tokens), jnp.float32),
            pltpu.VMEM((2, *blocks, CHUNK_WIDTH), bf16),
            dma((2 + CHUNKS,)),
            dma((CHUNKS, N_DP - 1)),
            dma((CHUNKS, N_DP - 1)),
            dma((N_DP - 1,)),
            dma((N_DP - 1,)),
            dma((CHUNKS, 2)),
            dma((CHUNKS, 2)),
            dma((2,)),
        ],
        compiler_params=pltpu.CompilerParams(
            collective_id=0, has_side_effects=True, vmem_limit_bytes=60 << 20
        ),
        name="balanced_attention",
    )(
        block_source,
        documents.reshape(-1),
        query_matrix.reshape(*blocks, width),
        key_matrix.reshape(*blocks, kv_width),
        value_matrix.reshape(*blocks, kv_width),
    )
    return attended.reshape(1, BLK_DEV * tokens, width)


def solution(mesh):
    placed = (P("dp", "sp", None), P("dp", "sp", None), P("dp", "sp", None), P(), P("dp", None))
    return jax.shard_map(
        on_device, mesh=mesh, in_specs=placed, out_specs=P("dp", "sp", None), check_vma=False
    )
```

time: 900 us -> 144 us (0.16)
  waiting for transfers between devices: 231 us -> 0 us
  matrix products: 217 us -> 0 us
  local copies, waits for them, and re-layouts: 159 us -> 9.15 us
  Pallas kernels: 0 us -> 135 us
  other arithmetic: 113 us -> 0 us
  blocking collectives: 101 us -> 0 us
  loops' own time: 40.7 us -> 0 us
  starting transfers between devices: 33.4 us -> 0 us
    all_to_all x6 -> x0, waiting for transfers between devices: 231 us -> none  [the longest x1 101 us: on_device(): lax.all_to_all(placed_q, 'sp', split_axis=2, concat_axis=0, tiled=True)]
    dot_general x96 -> x0, matrix products: 217 us -> none  [the longest x48 124 us: one_tile(): jnp.einsum('qhk,kd->qhd', weights.astype(jnp.bfloat16), value_tile, prefe...]
    pallas_call x0 -> x1, Pallas kernels: none -> 135 us  [on_device(): pl.pallas_call(fused_kernel, out_shape=jax.ShapeDtypeStruct((*blocks, wid...]
    all_to_all x1 -> x0, blocking collectives: 101 us -> none  [on_device(): lax.all_to_all(attended, 'sp', split_axis=0, concat_axis=1, tiled=True)]
    reduce_sum x49 -> x0, other arithmetic: 53.4 us -> none  [the longest x48 53.2 us: one_tile(): total = total * rescale + jnp.sum(weights, axis=-1)]
    gather x15 -> x0, local copies, waits for them, and re-layouts: 45 us -> none  [the longest x3 15.9 us: on_device(): query_matrix.reshape(block_list, BALANCE_TOKENS, QUERY_HEADS * HEAD_WIDTH)]
    another operation x17 -> x0, loops' own time: 40.7 us -> none  [the longest x1 37.1 us: attend(): return lax.fori_loop(0, query_count, one_block, empty)]
    dynamic_slice x114 -> x0, local copies, waits for them, and re-layouts: 38.6 us -> none  [the longest x32 23.7 us: one_block(): query_tile = lax.dynamic_slice_in_dim(query_seq, start, query_block, 0)]
  transfers between devices with their start and end apart: 6 -> 0, of which waited for: 5 -> 0; matrix products, arithmetic and copies ran while one was open for 12% -> 0% of each run, Pallas kernels for 0% -> 0%
where the time goes in v1:
time: 144 us
  Pallas kernels  135 us (94%)
  local copies, waits for them, and re-layouts  9.15 us (6%)
    pallas_call x1, Pallas kernels, on_device(): pl.pallas_call(fused_kernel, out_shape=jax.ShapeDtypeStruct((*blocks, wid...  135 us
    unnamed x2, local copies, waits for them, and re-layouts  9.15 us

profile of v1, /device:TPU:0, one launch (start us, length us, event | category | flops | bytes accessed | tf_op | source)
XLA Modules:
  0.0 143.7 jit_solution(3762303148908060057)
XLA Ops:
  0.0 1.4 copy.6.source_ref
  1.4 134.6 %balanced_attention.1 = bf16[4,128,8192]{2,1,0:T(8,128)(2,1)} custom-call(s32[32,16]{1,0:T(8,128)} %copy.6.source_ref, s32[128]{0:T(128)} %bitcast.9, bf16[4,128,8192]{2,1,0:T(8,128)(2,1)} %bitcast.6, bf16[4,128,1024]{2,1,0:T(8,128)(2,1)} %bitcast.7, bf16[4,128,1024]{2,1,0:T(8,128)(2,1)} %bitcast.8), custom_call_target="tpu_custom_call" | custom-call | tf_op jit(solution)/shard_map/balanced_attention/pallas_call | solution.py:265
  136.0 7.8 %copy.8 = bf16[1,512,8192]{2,1,0:T(8,128)(2,1)} copy(bf16[1,512,8192]{2,1,0:T(8,128)(2,1)} %bitcast.5) | data formatting | bytes 16777216

commit v2 on v1

v2 whole, which is shorter than its diff:
```python
import jax
import jax.numpy as jnp
from jax import lax
from jax.experimental import pallas as pl
from jax.experimental.pallas import tpu as pltpu
from jax.sharding import PartitionSpec as P

QUERY_HEADS = 64
KEY_VALUE_HEADS = 8
HEAD_WIDTH = 128
BALANCE_TOKENS = 128
MOST_BLK = 8
BLK_DEV = 4
N_DP = 4
N_SP = 32
GROUP = QUERY_HEADS // KEY_VALUE_HEADS
PART = 2
PARTS = QUERY_HEADS // PART
PART_WIDTH = PART * HEAD_WIDTH
PER_KV = GROUP // PART
HALO = MOST_BLK - 1
WINDOW = HALO + BLK_DEV
SPAN = MOST_BLK * BALANCE_TOKENS
MASKED = -1e30
LOG2E = 1.4426950408889634
MESH = pl.DeviceIdType.MESH


def fused_kernel(
    source_hbm,
    docs_ref,
    q_hbm,
    k_hbm,
    v_hbm,
    out_ref,
    source_ref,
    q_local,
    k_local,
    v_local,
    q_send,
    q_recv,
    kv_send,
    kv_recv,
    window,
    bias,
    load_sem,
    q_load_sem,
    q_send_sem,
    q_recv_sem,
    kv_send_sem,
    kv_recv_sem,
    halo_send_sem,
    halo_recv_sem,
):
    g = lax.axis_index("dp")
    s = lax.axis_index("sp")

    def dp_peer(step):
        return (lax.rem(g + step, N_DP), s)

    def sp_peer(step):
        return (g, lax.rem(s + step + N_SP, N_SP))

    source_load = pltpu.make_async_copy(source_hbm, source_ref, load_sem.at[0])
    k_load = pltpu.make_async_copy(k_hbm, k_local, load_sem.at[1])
    v_load = pltpu.make_async_copy(v_hbm, v_local, load_sem.at[2])
    source_load.start()
    k_load.start()
    v_load.start()

    def q_load(c):
        columns = pl.ds(c * GROUP * HEAD_WIDTH, GROUP * HEAD_WIDTH)
        return pltpu.make_async_copy(
            q_hbm.at[:, :, columns], q_local.at[:, :, columns], q_load_sem.at[c]
        )

    barrier = pltpu.get_barrier_semaphore()
    for step in range(1, N_DP):
        pl.semaphore_signal(barrier, 1, device_id=dp_peer(step), device_id_type=MESH)
    for step in (1, 2, -1, -2):
        pl.semaphore_signal(barrier, 1, device_id=sp_peer(step), device_id_type=MESH)

    source_load.wait()

    def departing(step):
        dest = lax.rem(g + step, N_DP)
        chosen = 0
        for slot in range(BLK_DEV):
            entry = source_ref[dest * BLK_DEV + slot, s]
            chosen = chosen + jnp.where((entry >> 2) == g, entry & 3, 0)
        return chosen

    def arrived_from(slot):
        entry = source_ref[g * BLK_DEV + slot, s]
        return (g - (entry >> 2)) & 3

    leaves = [departing(step) for step in range(N_DP)]
    comes = [arrived_from(slot) for slot in range(BLK_DEV)]

    def kv_copy(step):
        return pltpu.make_async_remote_copy(
            src_ref=kv_send.at[step - 1],
            dst_ref=kv_recv.at[step],
            send_sem=kv_send_sem.at[step - 1],
            recv_sem=kv_recv_sem.at[step - 1],
            device_id=dp_peer(step),
            device_id_type=MESH,
        )

    def q_copy(part, step):
        return pltpu.make_async_remote_copy(
            src_ref=q_send.at[part, step - 1],
            dst_ref=q_recv.at[part, step],
            send_sem=q_send_sem.at[part, step - 1],
            recv_sem=q_recv_sem.at[part, step - 1],
            device_id=dp_peer(step),
            device_id_type=MESH,
        )

    def near_copy(c):
        return pltpu.make_async_remote_copy(
            src_ref=window.at[c, pl.ds(HALO, BLK_DEV)],
            dst_ref=window.at[c, pl.ds(HALO - BLK_DEV, BLK_DEV)],
            send_sem=halo_send_sem.at[c, 0],
            recv_sem=halo_recv_sem.at[c, 0],
            device_id=sp_peer(1),
            device_id_type=MESH,
        )

    def far_copy(c):
        return pltpu.make_async_remote_copy(
            src_ref=window.at[c, pl.ds(WINDOW - (HALO - BLK_DEV), HALO - BLK_DEV)],
            dst_ref=window.at[c, pl.ds(0, HALO - BLK_DEV)],
            send_sem=halo_send_sem.at[c, 1],
            recv_sem=halo_recv_sem.at[c, 1],
            device_id=sp_peer(2),
            device_id_type=MESH,
        )

    k_load.wait()
    v_load.wait()
    for c in range(KEY_VALUE_HEADS):
        q_load(c).start()
    for step in (2, 1, 3, 0):
        target = kv_recv.at[0] if step == 0 else kv_send.at[step - 1]
        for c in range(KEY_VALUE_HEADS):
            columns = pl.ds(c * HEAD_WIDTH, HEAD_WIDTH)
            target[c, 0] = k_local[leaves[step], :, columns]
            target[c, 1] = v_local[leaves[step], :, columns]
        if step == 2:
            pl.semaphore_wait(barrier, 7)
        if step > 0:
            kv_copy(step).start()

    for c in range(KEY_VALUE_HEADS):
        q_load(c).wait()

    @pl.loop(0, PARTS)
    def _(part):
        columns = pl.ds(pl.multiple_of(part * PART_WIDTH, PART_WIDTH), PART_WIDTH)
        for step in (2, 1, 3):
            q_send[part, step - 1] = q_local[leaves[step], :, columns]
            q_copy(part, step).start()
        q_recv[part, 0] = q_local[leaves[0], :, columns]

    for slot in range(BLK_DEV):
        own = docs_ref[s * BLK_DEV + slot]
        for j in range(HALO):
            block = s * BLK_DEV + slot + j - HALO
            same = (docs_ref[jnp.maximum(block, 0)] == own) & (block >= 0)
            level = jnp.where(same, 0.0, MASKED).astype(jnp.float32)
            bias[slot, :, pl.ds(j * BALANCE_TOKENS, BALANCE_TOKENS)] = jnp.full(
                (8, BALANCE_TOKENS), level, jnp.float32
            )

    for step in range(1, N_DP):
        kv_copy(step).wait_recv()
    for slot in range(BLK_DEV):
        for c in range(KEY_VALUE_HEADS):
            window[c, HALO + slot] = kv_recv[comes[slot], c]

    @pl.loop(0, KEY_VALUE_HEADS)
    def _(c):
        near_copy(c).start()
        far_copy(c).start()

    row = lax.broadcasted_iota(jnp.int32, (BALANCE_TOKENS, BALANCE_TOKENS), 0)
    column = lax.broadcasted_iota(jnp.int32, (BALANCE_TOKENS, BALANCE_TOKENS), 1)
    triangle = jnp.where(column <= row, 0.0, MASKED).astype(jnp.float32)
    diagonal = jnp.concatenate([triangle] * PART, axis=0)
    factor = LOG2E * HEAD_WIDTH ** -0.5

    @pl.loop(0, PARTS)
    def _(part):
        c = part // PER_KV

        @pl.when(lax.rem(part, PER_KV) == 0)
        def _():
            near_copy(c).wait_recv()
            far_copy(c).wait_recv()

        for step in range(1, N_DP):
            q_copy(part, step).wait_recv()

        for slot in range(BLK_DEV):
            arrived = q_recv[part, 0]
            for step in range(1, N_DP):
                arrived = jnp.where(comes[slot] == step, q_recv[part, step], arrived)
            queries = jnp.concatenate(
                [arrived[:, h * HEAD_WIDTH : (h + 1) * HEAD_WIDTH] for h in range(PART)], axis=0
            )
            keys = window[c, pl.ds(slot, MOST_BLK), 0].reshape(SPAN, HEAD_WIDTH)
            values = window[c, pl.ds(slot, MOST_BLK), 1].reshape(SPAN, HEAD_WIDTH)
            level = bias[slot, pl.ds(0, 1)]
            scores = lax.dot_general(
                queries, keys, (((1,), (1,)), ((), ())), preferred_element_type=jnp.float32
            )
            far = scores[:, : HALO * BALANCE_TOKENS] + level
            near = scores[:, HALO * BALANCE_TOKENS :] + diagonal
            scores = jnp.concatenate([far, near], axis=1)
            top = jnp.max(scores, axis=1, keepdims=True)
            weights = jnp.exp2((scores - top) * factor)
            total = jnp.sum(weights, axis=1, keepdims=True)
            mixed = jnp.dot(
                weights.astype(jnp.bfloat16), values, preferred_element_type=jnp.float32
            )
            result = (mixed / total).astype(jnp.bfloat16)
            columns = pl.ds(pl.multiple_of(part * PART_WIDTH, PART_WIDTH), PART_WIDTH)
            out_ref[slot, :, columns] = jnp.concatenate(
                [result[h * BALANCE_TOKENS : (h + 1) * BALANCE_TOKENS] for h in range(PART)], axis=1
            )

    for step in range(1, N_DP):
        kv_copy(step).wait_send()

    @pl.loop(0, KEY_VALUE_HEADS)
    def _(c):
        near_copy(c).wait_send()
        far_copy(c).wait_send()

    @pl.loop(0, PARTS)
    def _(part):
        for step in range(1, N_DP):
            q_copy(part, step).wait_send()


def on_device(query_matrix, key_matrix, value_matrix, block_source, documents):
    bf16 = jnp.bfloat16
    tokens = BALANCE_TOKENS
    blocks = (BLK_DEV, tokens)
    dma = pltpu.SemaphoreType.DMA
    kv_width = KEY_VALUE_HEADS * HEAD_WIDTH
    width = QUERY_HEADS * HEAD_WIDTH
    smem = pl.BlockSpec(memory_space=pltpu.SMEM)
    anywhere = pl.BlockSpec(memory_space=pl.ANY)
    attended = pl.pallas_call(
        fused_kernel,
        out_shape=pltpu.VMEM((*blocks, width), bf16),
        in_specs=[anywhere, smem, anywhere, anywhere, anywhere],
        out_specs=pl.BlockSpec(memory_space=pltpu.VMEM),
        scratch_shapes=[
            pltpu.SMEM(block_source.shape[::-1], jnp.int32),
            pltpu.VMEM((*blocks, width), bf16),
            pltpu.VMEM((*blocks, kv_width), bf16),
            pltpu.VMEM((*blocks, kv_width), bf16),
            pltpu.VMEM((PARTS, N_DP - 1, tokens, PART_WIDTH), bf16),
            pltpu.VMEM((PARTS, N_DP, tokens, PART_WIDTH), bf16),
            pltpu.VMEM((N_DP - 1, KEY_VALUE_HEADS, 2, tokens, HEAD_WIDTH), bf16),
            pltpu.VMEM((N_DP, KEY_VALUE_HEADS, 2, tokens, HEAD_WIDTH), bf16),
            pltpu.VMEM((KEY_VALUE_HEADS, WINDOW, 2, tokens, HEAD_WIDTH), bf16),
            pltpu.VMEM((BLK_DEV, 8, HALO * tokens), jnp.float32),
            dma((3,)),
            dma((KEY_VALUE_HEADS,)),
            dma((PARTS, N_DP - 1)),
            dma((PARTS, N_DP - 1)),
            dma((N_DP - 1,)),
            dma((N_DP - 1,)),
            dma((KEY_VALUE_HEADS, 2)),
            dma((KEY_VALUE_HEADS, 2)),
        ],
        compiler_params=pltpu.CompilerParams(
            collective_id=0, has_side_effects=True, vmem_limit_bytes=48 << 20
        ),
        name="balanced_attention",
    )(
        block_source.T,
        documents.reshape(-1),
        query_matrix.reshape(*blocks, width),
        key_matrix.reshape(*blocks, kv_width),
        value_matrix.reshape(*blocks, kv_width),
    )
    return attended.reshape(1, BLK_DEV * tokens, width)


def solution(mesh):
    placed = (P("dp", "sp", None), P("dp", "sp", None), P("dp", "sp", None), P(), P("dp", None))
    return jax.shard_map(
        on_device, mesh=mesh, in_specs=placed, out_specs=P("dp", "sp", None), check_vma=False
    )
```

time: 144 us -> 132 us (0.917)
  Pallas kernels: 135 us -> 128 us
  local copies, waits for them, and re-layouts: 9.15 us -> 3.4 us
    pallas_call x1, Pallas kernels: 135 us -> 128 us  [on_device(): pl.pallas_call(fused_kernel, out_shape=pltpu.VMEM((*blocks, width), bf16)...]
    unnamed x2 -> x1, local copies, waits for them, and re-layouts: 9.15 us -> 3.4 us
where the time goes in v2:
time: 132 us; the launch traced here: 131 us
  Pallas kernels  128 us (97%)
  local copies, waits for them, and re-layouts  3.4 us (3%)
    pallas_call x1, Pallas kernels, on_device(): pl.pallas_call(fused_kernel, out_shape=pltpu.VMEM((*blocks, width), bf16)...  128 us
    unnamed x1, local copies, waits for them, and re-layouts  3.4 us

profile of v2, /device:TPU:0, one launch (start us, length us, event | category | flops | bytes accessed | tf_op | source)
XLA Modules:
  0.0 131.0 jit_solution(1586453131042612560)
XLA Ops:
  0.0 127.6 %balanced_attention.1 = bf16[4,128,8192]{2,1,0:T(8,128)(2,1)S(1)} custom-call(s32[16,32]{1,0:T(8,128)} %bitcast.10, s32[128]{0:T(128)} %bitcast.11, bf16[4,128,8192]{2,1,0:T(8,128)(2,1)} %bitcast.7, bf16[4,128,1024]{2,1,0:T(8,128)(2,1)} %bitcast.8, bf16[4,128,1024]{2,1,0:T(8,128)(2,1)} %bitcast.9), custom_call_target="tpu_custom_call" | custom-call | tf_op jit(solution)/shard_map/balanced_attention/pallas_call | solution.py:256
  127.6 3.4 %copy.7 = bf16[1,512,8192]{2,1,0:T(8,128)(2,1)} copy(bf16[1,512,8192]{2,1,0:T(8,128)(2,1)S(1)} %bitcast.6) | data formatting | bytes 16777216

commit v3 on v2

--- a/solution.py
+++ b/solution.py
@@ -18,6 +18,9 @@
 PARTS = QUERY_HEADS // PART
 PART_WIDTH = PART * HEAD_WIDTH
 PER_KV = GROUP // PART
+PIECES = 4
+PIECE_HEADS = KEY_VALUE_HEADS // PIECES
+PIECE_WIDTH = PIECE_HEADS * HEAD_WIDTH
 HALO = MOST_BLK - 1
 WINDOW = HALO + BLK_DEV
 SPAN = MOST_BLK * BALANCE_TOKENS
@@ -51,6 +54,7 @@
     kv_recv_sem,
     halo_send_sem,
     halo_recv_sem,
+    ready,
 ):
     g = lax.axis_index("dp")
     s = lax.axis_index("sp")
@@ -59,14 +63,22 @@
         return (lax.rem(g + step, N_DP), s)
 
     def sp_peer(step):
-        return (g, lax.rem(s + step + N_SP, N_SP))
+        return (g, lax.rem(s + step, N_SP))
 
     source_load = pltpu.make_async_copy(source_hbm, source_ref, load_sem.at[0])
-    k_load = pltpu.make_async_copy(k_hbm, k_local, load_sem.at[1])
-    v_load = pltpu.make_async_copy(v_hbm, v_local, load_sem.at[2])
+
+    def kv_load(kind, piece):
+        columns = pl.ds(piece * PIECE_WIDTH, PIECE_WIDTH)
+        return pltpu.make_async_copy(
+            (k_hbm, v_hbm)[kind].at[:, :, columns],
+            (k_local, v_local)[kind][piece],
+            load_sem.at[1 + 2 * piece + kind],
+        )
+
     source_load.start()
-    k_load.start()
-    v_load.start()
+    for piece in range(PIECES):
+        kv_load(0, piece).start()
+        kv_load(1, piece).start()
 
     def q_load(c):
         columns = pl.ds(c * GROUP * HEAD_WIDTH, GROUP * HEAD_WIDTH)
@@ -77,8 +89,52 @@
     barrier = pltpu.get_barrier_semaphore()
     for step in range(1, N_DP):
         pl.semaphore_signal(barrier, 1, device_id=dp_peer(step), device_id_type=MESH)
-    for step in (1, 2, -1, -2):
-        pl.semaphore_signal(barrier, 1, device_id=sp_peer(step), device_id_type=MESH)
+
+    def greet(semaphore, column):
+        pl.semaphore_signal(semaphore, 1, device_id=(g, column), device_id_type=MESH)
+
+    @pl.when((s == 1) | (s >= 3))
+    def _():
+        greet(barrier, s - 1)
+
+    @pl.when(s >= 4)
+    def _():
+        greet(barrier, s - 2)
+
+    def enter():
+        @pl.when(s == 0)
+        def _():
+            pl.semaphore_wait(barrier, 4)
+            greet(barrier, 2)
+
+        @pl.when(s == 1)
+        def _():
+            pl.semaphore_wait(barrier, 3)
+            greet(barrier, 2)
+            greet(barrier, 3)
+
+        @pl.when(s == 2)
+        def _():
+            pl.semaphore_wait(barrier, 7)
+            greet(ready, 0)
+            greet(ready, 1)
+
+        @pl.when(s == 3)
+        def _():
+            pl.semaphore_wait(barrier, 6)
+            greet(ready, 1)
+
+        @pl.when((s >= 4) & (s <= N_SP - 3))
+        def _():
+            pl.semaphore_wait(barrier, 5)
+
+        @pl.when(s == N_SP - 2)
+        def _():
+            pl.semaphore_wait(barrier, 4)
+
+        @pl.when(s == N_SP - 1)
+        def _():
+            pl.semaphore_wait(barrier, 3)
 
     source_load.wait()
 
@@ -97,12 +153,20 @@
     leaves = [departing(step) for step in range(N_DP)]
     comes = [arrived_from(slot) for slot in range(BLK_DEV)]
 
-    def kv_copy(step):
+    def turns(turn, number):
+        if turn >= 2:
+            step = (2, 0)[turn - 2]
+            return step, leaves[step]
+        step = 1 + 2 * lax.rem(s + number + turn, 2)
+        return step, jnp.where(step == 1, leaves[1], leaves[3])
+
+    def kv_copy(piece, step):
+        heads = pl.ds(piece * PIECE_HEADS, PIECE_HEADS)
         return pltpu.make_async_remote_copy(
-            src_ref=kv_send.at[step - 1],
-            dst_ref=kv_recv.at[step],
-            send_sem=kv_send_sem.at[step - 1],
-            recv_sem=kv_recv_sem.at[step - 1],
+            src_ref=kv_send.at[step - 1, heads],
+            dst_ref=kv_recv.at[step, heads],
+            send_sem=kv_send_sem.at[piece, step - 1],
+            recv_sem=kv_recv_sem.at[piece, step - 1],
             device_id=dp_peer(step),
             device_id_type=MESH,
         )
@@ -137,20 +201,28 @@
             device_id_type=MESH,
         )
 
-    k_load.wait()
-    v_load.wait()
-    for c in range(KEY_VALUE_HEADS):
-        q_load(c).start()
-    for step in (2, 1, 3, 0):
-        target = kv_recv.at[0] if step == 0 else kv_send.at[step - 1]
-        for c in range(KEY_VALUE_HEADS):
-            columns = pl.ds(c * HEAD_WIDTH, HEAD_WIDTH)
-            target[c, 0] = k_local[leaves[step], :, columns]
-            target[c, 1] = v_local[leaves[step], :, columns]
-        if step == 2:
-            pl.semaphore_wait(barrier, 7)
-        if step > 0:
-            kv_copy(step).start()
+    for piece in range(PIECES):
+        kv_load(0, piece).wait()
+        kv_load(1, piece).wait()
+        if piece == PIECES - 1:
+            for c in range(KEY_VALUE_HEADS):
+                q_load(c).start()
+        for turn in range(N_DP):
+            step, leaf = turns(turn, piece)
+            for head in range(PIECE_HEADS):
+                columns = pl.ds(head * HEAD_WIDTH, HEAD_WIDTH)
+                key = k_local[piece][leaf, :, columns]
+                value = v_local[piece][leaf, :, columns]
+                if turn < N_DP - 1:
+                    kv_send[step - 1, piece * PIECE_HEADS + head, 0] = key
+                    kv_send[step - 1, piece * PIECE_HEADS + head, 1] = value
+                else:
+                    kv_recv[0, piece * PIECE_HEADS + head, 0] = key
+                    kv_recv[0, piece * PIECE_HEADS + head, 1] = value
+            if piece == 0 and turn == 0:
+                enter()
+            if turn < N_DP - 1:
+                kv_copy(piece, step).start()
 
     for c in range(KEY_VALUE_HEADS):
         q_load(c).wait()
@@ -158,8 +230,9 @@
     @pl.loop(0, PARTS)
     def _(part):
         columns = pl.ds(pl.multiple_of(part * PART_WIDTH, PART_WIDTH), PART_WIDTH)
-        for step in (2, 1, 3):
-            q_send[part, step - 1] = q_local[leaves[step], :, columns]
+        for turn in range(N_DP - 1):
+            step, leaf = turns(turn, part)
+            q_send[part, step - 1] = q_local[leaf, :, columns]
             q_copy(part, step).start()
         q_recv[part, 0] = q_local[leaves[0], :, columns]
 
@@ -173,16 +246,54 @@
                 (8, BALANCE_TOKENS), level, jnp.float32
             )
 
-    for step in range(1, N_DP):
-        kv_copy(step).wait_recv()
+    for piece in range(PIECES):
+        for step in range(1, N_DP):
+            kv_copy(piece, step).wait_recv()
     for slot in range(BLK_DEV):
         for c in range(KEY_VALUE_HEADS):
             window[c, HALO + slot] = kv_recv[comes[slot], c]
 
-    @pl.loop(0, KEY_VALUE_HEADS)
-    def _(c):
-        near_copy(c).start()
-        far_copy(c).start()
+    def each_halo(near_act, far_act, near_when, far_when):
+        @pl.when(near_when)
+        def _():
+            @pl.loop(0, KEY_VALUE_HEADS)
+            def _(c):
+                near_act(c)
+
+                @pl.when(far_when)
+                def _():
+                    far_act(c)
+
+    @pl.when(s == 0)
+    def _():
+        pl.semaphore_wait(ready, 1)
+
+    @pl.when(s == 1)
+    def _():
+        pl.semaphore_wait(ready, 2)
+
+    each_halo(
+        lambda c: near_copy(c).start(),
+        lambda c: far_copy(c).start(),
+        s < N_SP - 1,
+        s < N_SP - 2,
+    )
+
+    @pl.when(s < 2)
+    def _():
+        @pl.loop(0, KEY_VALUE_HEADS)
+        def _(c):
+            window[c, pl.ds(0, HALO - BLK_DEV)] = jnp.zeros(
+                (HALO - BLK_DEV, 2, BALANCE_TOKENS, HEAD_WIDTH), jnp.bfloat16
+            )
+
+    @pl.when(s < 1)
+    def _():
+        @pl.loop(0, KEY_VALUE_HEADS)
+        def _(c):
+            window[c, pl.ds(HALO - BLK_DEV, BLK_DEV)] = jnp.zeros(
+                (BLK_DEV, 2, BALANCE_TOKENS, HEAD_WIDTH), jnp.bfloat16
+            )
 
     row = lax.broadcasted_iota(jnp.int32, (BALANCE_TOKENS, BALANCE_TOKENS), 0)
     column = lax.broadcasted_iota(jnp.int32, (BALANCE_TOKENS, BALANCE_TOKENS), 1)
@@ -194,9 +305,12 @@
     def _(part):
         c = part // PER_KV
 
-        @pl.when(lax.rem(part, PER_KV) == 0)
+        @pl.when((lax.rem(part, PER_KV) == 0) & (s >= 1))
         def _():
             near_copy(c).wait_recv()
+
+        @pl.when((lax.rem(part, PER_KV) == 0) & (s >= 2))
+        def _():
             far_copy(c).wait_recv()
 
         for step in range(1, N_DP):
@@ -211,6 +325,7 @@
             )
             keys = window[c, pl.ds(slot, MOST_BLK), 0].reshape(SPAN, HEAD_WIDTH)
             values = window[c, pl.ds(slot, MOST_BLK), 1].reshape(SPAN, HEAD_WIDTH)
+            widened = jnp.concatenate([values, jnp.ones_like(values)], axis=1)
             level = bias[slot, pl.ds(0, 1)]
             scores = lax.dot_general(
                 queries, keys, (((1,), (1,)), ((), ())), preferred_element_type=jnp.float32
@@ -220,23 +335,25 @@
             scores = jnp.concatenate([far, near], axis=1)
             top = jnp.max(scores, axis=1, keepdims=True)
             weights = jnp.exp2((scores - top) * factor)
-            total = jnp.sum(weights, axis=1, keepdims=True)
             mixed = jnp.dot(
-                weights.astype(jnp.bfloat16), values, preferred_element_type=jnp.float32
-            )
-            result = (mixed / total).astype(jnp.bfloat16)
+                weights.astype(jnp.bfloat16), widened, preferred_element_type=jnp.float32
+            )
+            result = (mixed[:, :HEAD_WIDTH] / mixed[:, HEAD_WIDTH:]).astype(jnp.bfloat16)
             columns = pl.ds(pl.multiple_of(part * PART_WIDTH, PART_WIDTH), PART_WIDTH)
             out_ref[slot, :, columns] = jnp.concatenate(
                 [result[h * BALANCE_TOKENS : (h + 1) * BALANCE_TOKENS] for h in range(PART)], axis=1
             )
 
-    for step in range(1, N_DP):
-        kv_copy(step).wait_send()
-
-    @pl.loop(0, KEY_VALUE_HEADS)
-    def _(c):
-        near_copy(c).wait_send()
-        far_copy(c).wait_send()
+    for piece in range(PIECES):
+        for step in range(1, N_DP):
+            kv_copy(piece, step).wait_send()
+
+    each_halo(
+        lambda c: near_copy(c).wait_send(),
+        lambda c: far_copy(c).wait_send(),
+        s < N_SP - 1,
+        s < N_SP - 2,
+    )
 
     @pl.loop(0, PARTS)
     def _(part):
@@ -261,22 +378,23 @@
         scratch_shapes=[
             pltpu.SMEM(block_source.shape[::-1], jnp.int32),
             pltpu.VMEM((*blocks, width), bf16),
-            pltpu.VMEM((*blocks, kv_width), bf16),
-            pltpu.VMEM((*blocks, kv_width), bf16),
+            [pltpu.VMEM((*blocks, PIECE_WIDTH), bf16)] * PIECES,
+            [pltpu.VMEM((*blocks, PIECE_WIDTH), bf16)] * PIECES,
             pltpu.VMEM((PARTS, N_DP - 1, tokens, PART_WIDTH), bf16),
             pltpu.VMEM((PARTS, N_DP, tokens, PART_WIDTH), bf16),
             pltpu.VMEM((N_DP - 1, KEY_VALUE_HEADS, 2, tokens, HEAD_WIDTH), bf16),
             pltpu.VMEM((N_DP, KEY_VALUE_HEADS, 2, tokens, HEAD_WIDTH), bf16),
             pltpu.VMEM((KEY_VALUE_HEADS, WINDOW, 2, tokens, HEAD_WIDTH), bf16),
             pltpu.VMEM((BLK_DEV, 8, HALO * tokens), jnp.float32),
-            dma((3,)),
+            dma((1 + 2 * PIECES,)),
             dma((KEY_VALUE_HEADS,)),
             dma((PARTS, N_DP - 1)),
             dma((PARTS, N_DP - 1)),
-            dma((N_DP - 1,)),
-            dma((N_DP - 1,)),
+            dma((PIECES, N_DP - 1)),
+            dma((PIECES, N_DP - 1)),
             dma((KEY_VALUE_HEADS, 2)),
             dma((KEY_VALUE_HEADS, 2)),
+            pltpu.SemaphoreType.REGULAR,
         ],
         compiler_params=pltpu.CompilerParams(
             collective_id=0, has_side_effects=True, vmem_limit_bytes=48 << 20

time: 132 us -> 127 us (0.962)
  Pallas kernels: 128 us -> 123 us
    pallas_call x1, Pallas kernels: 128 us -> 123 us  [on_device(): pl.pallas_call(fused_kernel, out_shape=pltpu.VMEM((*blocks, width), bf16)...]
where the time goes in v3:
time: 127 us; the launch traced here: 126 us
  Pallas kernels  123 us (97%)
  local copies, waits for them, and re-layouts  3.4 us (3%)
    pallas_call x1, Pallas kernels, on_device(): pl.pallas_call(fused_kernel, out_shape=pltpu.VMEM((*blocks, width), bf16)...  123 us
    unnamed x1, local copies, waits for them, and re-layouts  3.4 us

profile of v3, /device:TPU:0, one launch (start us, length us, event | category | flops | bytes accessed | tf_op | source)
XLA Modules:
  0.0 126.0 jit_solution(7859219191452834740)
XLA Ops:
  0.0 122.6 %balanced_attention.1 = bf16[4,128,8192]{2,1,0:T(8,128)(2,1)S(1)} custom-call(s32[16,32]{1,0:T(8,128)} %bitcast.10, s32[128]{0:T(128)} %bitcast.11, bf16[4,128,8192]{2,1,0:T(8,128)(2,1)} %bitcast.7, bf16[4,128,1024]{2,1,0:T(8,128)(2,1)} %bitcast.8, bf16[4,128,1024]{2,1,0:T(8,128)(2,1)} %bitcast.9), custom_call_target="tpu_custom_call" | custom-call | tf_op jit(solution)/shard_map/balanced_attention/pallas_call | solution.py:373
  122.6 3.4 %copy.7 = bf16[1,512,8192]{2,1,0:T(8,128)(2,1)} copy(bf16[1,512,8192]{2,1,0:T(8,128)(2,1)S(1)} %bitcast.6) | data formatting | bytes 16777216

commit v4 on v3

--- a/solution.py
+++ b/solution.py
@@ -14,11 +14,14 @@
 N_DP = 4
 N_SP = 32
 GROUP = QUERY_HEADS // KEY_VALUE_HEADS
-PART = 2
-PARTS = QUERY_HEADS // PART
-PART_WIDTH = PART * HEAD_WIDTH
-PER_KV = GROUP // PART
-PIECES = 4
+PAIR = 2
+WHOLE = KEY_VALUE_HEADS - 2
+HALF = GROUP // 2
+LAST = KEY_VALUE_HEADS - 1
+PAIRS = GROUP // PAIR - 1
+SINGLES = 2
+GROUPS = WHOLE + 2 + PAIRS + SINGLES
+PIECES = 2
 PIECE_HEADS = KEY_VALUE_HEADS // PIECES
 PIECE_WIDTH = PIECE_HEADS * HEAD_WIDTH
 HALO = MOST_BLK - 1
@@ -171,15 +174,33 @@
             device_id_type=MESH,
         )
 
-    def q_copy(part, step):
+    def q_copy(group, first, count, step):
+        heads = pl.ds(first, count)
         return pltpu.make_async_remote_copy(
-            src_ref=q_send.at[part, step - 1],
-            dst_ref=q_recv.at[part, step],
-            send_sem=q_send_sem.at[part, step - 1],
-            recv_sem=q_recv_sem.at[part, step - 1],
+            src_ref=q_send.at[step - 1, heads],
+            dst_ref=q_recv.at[step, heads],
+            send_sem=q_send_sem.at[group, step - 1],
+            recv_sem=q_recv_sem.at[group, step - 1],
             device_id=dp_peer(step),
             device_id_type=MESH,
         )
+
+    def each_group(act):
+        @pl.loop(0, WHOLE)
+        def _(c):
+            act(c, c * GROUP, GROUP)
+
+        @pl.loop(0, 2)
+        def _(i):
+            act(WHOLE + i, WHOLE * GROUP + i * HALF, HALF)
+
+        @pl.loop(0, PAIRS)
+        def _(i):
+            act(WHOLE + 2 + i, LAST * GROUP + i * PAIR, PAIR)
+
+        @pl.loop(0, SINGLES)
+        def _(i):
+            act(GROUPS - SINGLES + i, QUERY_HEADS - SINGLES + i, 1)
 
     def near_copy(c):
         return pltpu.make_async_remote_copy(
@@ -227,14 +248,21 @@
     for c in range(KEY_VALUE_HEADS):
         q_load(c).wait()
 
-    @pl.loop(0, PARTS)
-    def _(part):
-        columns = pl.ds(pl.multiple_of(part * PART_WIDTH, PART_WIDTH), PART_WIDTH)
-        for turn in range(N_DP - 1):
-            step, leaf = turns(turn, part)
-            q_send[part, step - 1] = q_local[leaf, :, columns]
-            q_copy(part, step).start()
-        q_recv[part, 0] = q_local[leaves[0], :, columns]
+    def send_group(group, first, count):
+        for turn in range(N_DP):
+            step, leaf = turns(turn, group)
+            for i in range(count):
+                head = first + i
+                columns = pl.ds(pl.multiple_of(head * HEAD_WIDTH, HEAD_WIDTH), HEAD_WIDTH)
+                block = q_local[leaf, :, columns]
+                if turn < N_DP - 1:
+                    q_send[step - 1, head] = block
+                else:
+                    q_recv[0, head] = block
+            if turn < N_DP - 1:
+                q_copy(group, first, count, step).start()
+
+    each_group(send_group)
 
     for slot in range(BLK_DEV):
         own = docs_ref[s * BLK_DEV + slot]
@@ -298,31 +326,16 @@
     row = lax.broadcasted_iota(jnp.int32, (BALANCE_TOKENS, BALANCE_TOKENS), 0)
     column = lax.broadcasted_iota(jnp.int32, (BALANCE_TOKENS, BALANCE_TOKENS), 1)
     triangle = jnp.where(column <= row, 0.0, MASKED).astype(jnp.float32)
-    diagonal = jnp.concatenate([triangle] * PART, axis=0)
     factor = LOG2E * HEAD_WIDTH ** -0.5
 
-    @pl.loop(0, PARTS)
-    def _(part):
-        c = part // PER_KV
-
-        @pl.when((lax.rem(part, PER_KV) == 0) & (s >= 1))
-        def _():
-            near_copy(c).wait_recv()
-
-        @pl.when((lax.rem(part, PER_KV) == 0) & (s >= 2))
-        def _():
-            far_copy(c).wait_recv()
-
-        for step in range(1, N_DP):
-            q_copy(part, step).wait_recv()
-
+    def attend(c, first, count):
+        heads = pl.ds(first, count)
+        diagonal = jnp.concatenate([triangle] * count, axis=0)
         for slot in range(BLK_DEV):
-            arrived = q_recv[part, 0]
+            arrived = q_recv[0, heads]
             for step in range(1, N_DP):
-                arrived = jnp.where(comes[slot] == step, q_recv[part, step], arrived)
-            queries = jnp.concatenate(
-                [arrived[:, h * HEAD_WIDTH : (h + 1) * HEAD_WIDTH] for h in range(PART)], axis=0
-            )
+                arrived = jnp.where(comes[slot] == step, q_recv[step, heads], arrived)
+            queries = arrived.reshape(count * BALANCE_TOKENS, HEAD_WIDTH)
             keys = window[c, pl.ds(slot, MOST_BLK), 0].reshape(SPAN, HEAD_WIDTH)
             values = window[c, pl.ds(slot, MOST_BLK), 1].reshape(SPAN, HEAD_WIDTH)
             widened = jnp.concatenate([values, jnp.ones_like(values)], axis=1)
@@ -339,10 +352,55 @@
                 weights.astype(jnp.bfloat16), widened, preferred_element_type=jnp.float32
             )
             result = (mixed[:, :HEAD_WIDTH] / mixed[:, HEAD_WIDTH:]).astype(jnp.bfloat16)
-            columns = pl.ds(pl.multiple_of(part * PART_WIDTH, PART_WIDTH), PART_WIDTH)
+            width = count * HEAD_WIDTH
+            columns = pl.ds(pl.multiple_of(first * HEAD_WIDTH, width), width)
             out_ref[slot, :, columns] = jnp.concatenate(
-                [result[h * BALANCE_TOKENS : (h + 1) * BALANCE_TOKENS] for h in range(PART)], axis=1
-            )
+                [result[h * BALANCE_TOKENS : (h + 1) * BALANCE_TOKENS] for h in range(count)], axis=1
+            )
+
+    def await_group(group, first, count):
+        for step in range(1, N_DP):
+            q_copy(group, first, count, step).wait_recv()
+
+    def await_halo(c):
+        @pl.when(s >= 1)
+        def _():
+            near_copy(c).wait_recv()
+
+        @pl.when(s >= 2)
+        def _():
+            far_copy(c).wait_recv()
+
+    @pl.loop(0, WHOLE)
+    def _(c):
+        await_halo(c)
+        await_group(c, c * GROUP, GROUP)
+
+        @pl.loop(0, GROUP // PAIR)
+        def _(i):
+            attend(c, c * GROUP + i * PAIR, PAIR)
+
+    await_halo(WHOLE)
+
+    @pl.loop(0, 2)
+    def _(i):
+        await_group(WHOLE + i, WHOLE * GROUP + i * HALF, HALF)
+
+        @pl.loop(0, HALF // PAIR)
+        def _(j):
+            attend(WHOLE, WHOLE * GROUP + i * HALF + j * PAIR, PAIR)
+
+    await_halo(LAST)
+
+    @pl.loop(0, PAIRS)
+    def _(i):
+        await_group(WHOLE + 2 + i, LAST * GROUP + i * PAIR, PAIR)
+        attend(LAST, LAST * GROUP + i * PAIR, PAIR)
+
+    @pl.loop(0, SINGLES)
+    def _(i):
+        await_group(GROUPS - SINGLES + i, QUERY_HEADS - SINGLES + i, 1)
+        attend(LAST, QUERY_HEADS - SINGLES + i, 1)
 
     for piece in range(PIECES):
         for step in range(1, N_DP):
@@ -355,10 +413,11 @@
         s < N_SP - 2,
     )
 
-    @pl.loop(0, PARTS)
-    def _(part):
+    def sent_group(group, first, count):
         for step in range(1, N_DP):
-            q_copy(part, step).wait_send()
+            q_copy(group, first, count, step).wait_send()
+
+    each_group(sent_group)
 
 
 def on_device(query_matrix, key_matrix, value_matrix, block_source, documents):
@@ -380,16 +439,16 @@
             pltpu.VMEM((*blocks, width), bf16),
             [pltpu.VMEM((*blocks, PIECE_WIDTH), bf16)] * PIECES,
             [pltpu.VMEM((*blocks, PIECE_WIDTH), bf16)] * PIECES,
-            pltpu.VMEM((PARTS, N_DP - 1, tokens, PART_WIDTH), bf16),
-            pltpu.VMEM((PARTS, N_DP, tokens, PART_WIDTH), bf16),
+            pltpu.VMEM((N_DP - 1, QUERY_HEADS, tokens, HEAD_WIDTH), bf16),
+            pltpu.VMEM((N_DP, QUERY_HEADS, tokens, HEAD_WIDTH), bf16),
             pltpu.VMEM((N_DP - 1, KEY_VALUE_HEADS, 2, tokens, HEAD_WIDTH), bf16),
             pltpu.VMEM((N_DP, KEY_VALUE_HEADS, 2, tokens, HEAD_WIDTH), bf16),
             pltpu.VMEM((KEY_VALUE_HEADS, WINDOW, 2, tokens, HEAD_WIDTH), bf16),
             pltpu.VMEM((BLK_DEV, 8, HALO * tokens), jnp.float32),
             dma((1 + 2 * PIECES,)),
             dma((KEY_VALUE_HEADS,)),
-            dma((PARTS, N_DP - 1)),
-            dma((PARTS, N_DP - 1)),
+            dma((GROUPS, N_DP - 1)),
+            dma((GROUPS, N_DP - 1)),
             dma((PIECES, N_DP - 1)),
             dma((PIECES, N_DP - 1)),
             dma((KEY_VALUE_HEADS, 2)),

time: 127 us -> 126 us (level)
  no operation moved by 1% of the time
where the time goes in v4:
time: 126 us; the launch traced here: 125 us
  Pallas kernels  122 us (97%)
  local copies, waits for them, and re-layouts  3.4 us (3%)
    pallas_call x1, Pallas kernels, on_device(): pl.pallas_call(fused_kernel, out_shape=pltpu.VMEM((*blocks, width), bf16)...  122 us
    unnamed x1, local copies, waits for them, and re-layouts  3.4 us

profile of v4, /device:TPU:0, one launch (start us, length us, event | category | flops | bytes accessed | tf_op | source)
XLA Modules:
  0.0 125.4 jit_solution(4997073588181435327)
XLA Ops:
  0.0 122.0 %balanced_attention.1 = bf16[4,128,8192]{2,1,0:T(8,128)(2,1)S(1)} custom-call(s32[16,32]{1,0:T(8,128)} %bitcast.10, s32[128]{0:T(128)} %bitcast.11, bf16[4,128,8192]{2,1,0:T(8,128)(2,1)} %bitcast.7, bf16[4,128,1024]{2,1,0:T(8,128)(2,1)} %bitcast.8, bf16[4,128,1024]{2,1,0:T(8,128)(2,1)} %bitcast.9), custom_call_target="tpu_custom_call" | custom-call | tf_op jit(solution)/shard_map/balanced_attention/pallas_call | solution.py:432
  122.0 3.4 %copy.7 = bf16[1,512,8192]{2,1,0:T(8,128)(2,1)} copy(bf16[1,512,8192]{2,1,0:T(8,128)(2,1)S(1)} %bitcast.6) | data formatting | bytes 16777216

commit v5 on v4

--- a/solution.py
+++ b/solution.py
@@ -19,8 +19,10 @@
 HALF = GROUP // 2
 LAST = KEY_VALUE_HEADS - 1
 PAIRS = GROUP // PAIR - 1
-SINGLES = 2
-GROUPS = WHOLE + 2 + PAIRS + SINGLES
+GROUPS = WHOLE + 2 + PAIRS + 1
+TAIL = QUERY_HEADS - PAIR
+TAIL_WIDTH = PAIR * HEAD_WIDTH
+READY_WIDTH = TAIL * HEAD_WIDTH
 PIECES = 2
 PIECE_HEADS = KEY_VALUE_HEADS // PIECES
 PIECE_WIDTH = PIECE_HEADS * HEAD_WIDTH
@@ -32,6 +34,60 @@
 MESH = pl.DeviceIdType.MESH
 
 
+def causal_levels():
+    row = lax.broadcasted_iota(jnp.int32, (BALANCE_TOKENS, BALANCE_TOKENS), 0)
+    column = lax.broadcasted_iota(jnp.int32, (BALANCE_TOKENS, BALANCE_TOKENS), 1)
+    triangle = jnp.where(column <= row, 0.0, MASKED).astype(jnp.float32)
+    return jnp.concatenate([triangle] * PAIR, axis=0)
+
+
+def attend_pair(queries, keys, values, level, diagonal):
+    factor = LOG2E * HEAD_WIDTH ** -0.5
+    widened = jnp.concatenate([values, jnp.ones_like(values)], axis=1)
+    scores = lax.dot_general(
+        queries, keys, (((1,), (1,)), ((), ())), preferred_element_type=jnp.float32
+    )
+    far = scores[:, : HALO * BALANCE_TOKENS] + level
+    near = scores[:, HALO * BALANCE_TOKENS :] + diagonal
+    scores = jnp.concatenate([far, near], axis=1)
+    top = jnp.max(scores, axis=1, keepdims=True)
+    weights = jnp.exp2((scores - top) * factor)
+    mixed = jnp.dot(weights.astype(jnp.bfloat16), widened, preferred_element_type=jnp.float32)
+    result = (mixed[:, :HEAD_WIDTH] / mixed[:, HEAD_WIDTH:]).astype(jnp.bfloat16)
+    return jnp.concatenate(
+        [result[h * BALANCE_TOKENS : (h + 1) * BALANCE_TOKENS] for h in range(PAIR)], axis=1
+    )
+
+
+def finish_kernel(ready_ref, queries_ref, window_ref, bias_ref, out_hbm, staged, sem):
+    copies = [
+        pltpu.make_async_copy(
+            ready_ref.at[slot, :, pl.ds(0, READY_WIDTH)],
+            out_hbm.at[slot, :, pl.ds(0, READY_WIDTH)],
+            sem.at[slot],
+        )
+        for slot in range(BLK_DEV)
+    ]
+    for copy in copies:
+        copy.start()
+    diagonal = causal_levels()
+    for slot in range(BLK_DEV):
+        staged[slot] = attend_pair(
+            queries_ref[slot],
+            window_ref[pl.ds(slot, MOST_BLK), 0].reshape(SPAN, HEAD_WIDTH),
+            window_ref[pl.ds(slot, MOST_BLK), 1].reshape(SPAN, HEAD_WIDTH),
+            bias_ref[slot, pl.ds(0, 1)],
+            diagonal,
+        )
+    last = pltpu.make_async_copy(
+        staged, out_hbm.at[:, :, pl.ds(READY_WIDTH, TAIL_WIDTH)], sem.at[BLK_DEV]
+    )
+    last.start()
+    for copy in copies:
+        copy.wait()
+    last.wait()
+
+
 def fused_kernel(
     source_hbm,
     docs_ref,
@@ -39,6 +95,9 @@
     k_hbm,
     v_hbm,
     out_ref,
+    tail_queries,
+    tail_window,
+    bias,
     source_ref,
     q_local,
     k_local,
@@ -48,7 +107,6 @@
     kv_send,
     kv_recv,
     window,
-    bias,
     load_sem,
     q_load_sem,
     q_send_sem,
@@ -194,13 +252,10 @@
         def _(i):
             act(WHOLE + i, WHOLE * GROUP + i * HALF, HALF)
 
-        @pl.loop(0, PAIRS)
+        @pl.loop(0, PAIRS + 1)
         def _(i):
             act(WHOLE + 2 + i, LAST * GROUP + i * PAIR, PAIR)
 
-        @pl.loop(0, SINGLES)
-        def _(i):
-            act(GROUPS - SINGLES + i, QUERY_HEADS - SINGLES + i, 1)
 
     def near_copy(c):
         return pltpu.make_async_remote_copy(
@@ -323,39 +378,24 @@
                 (BLK_DEV, 2, BALANCE_TOKENS, HEAD_WIDTH), jnp.bfloat16
             )
 
-    row = lax.broadcasted_iota(jnp.int32, (BALANCE_TOKENS, BALANCE_TOKENS), 0)
-    column = lax.broadcasted_iota(jnp.int32, (BALANCE_TOKENS, BALANCE_TOKENS), 1)
-    triangle = jnp.where(column <= row, 0.0, MASKED).astype(jnp.float32)
-    factor = LOG2E * HEAD_WIDTH ** -0.5
-
-    def attend(c, first, count):
+    def slot_queries(slot, first, count):
         heads = pl.ds(first, count)
-        diagonal = jnp.concatenate([triangle] * count, axis=0)
+        arrived = q_recv[0, heads]
+        for step in range(1, N_DP):
+            arrived = jnp.where(comes[slot] == step, q_recv[step, heads], arrived)
+        return arrived.reshape(count * BALANCE_TOKENS, HEAD_WIDTH)
+
+    diagonal = causal_levels()
+
+    def attend(c, first):
         for slot in range(BLK_DEV):
-            arrived = q_recv[0, heads]
-            for step in range(1, N_DP):
-                arrived = jnp.where(comes[slot] == step, q_recv[step, heads], arrived)
-            queries = arrived.reshape(count * BALANCE_TOKENS, HEAD_WIDTH)
-            keys = window[c, pl.ds(slot, MOST_BLK), 0].reshape(SPAN, HEAD_WIDTH)
-            values = window[c, pl.ds(slot, MOST_BLK), 1].reshape(SPAN, HEAD_WIDTH)
-            widened = jnp.concatenate([values, jnp.ones_like(values)], axis=1)
-            level = bias[slot, pl.ds(0, 1)]
-            scores = lax.dot_general(
-                queries, keys, (((1,), (1,)), ((), ())), preferred_element_type=jnp.float32
-            )
-            far = scores[:, : HALO * BALANCE_TOKENS] + level
-            near = scores[:, HALO * BALANCE_TOKENS :] + diagonal
-            scores = jnp.concatenate([far, near], axis=1)
-            top = jnp.max(scores, axis=1, keepdims=True)
-            weights = jnp.exp2((scores - top) * factor)
-            mixed = jnp.dot(
-                weights.astype(jnp.bfloat16), widened, preferred_element_type=jnp.float32
-            )
-            result = (mixed[:, :HEAD_WIDTH] / mixed[:, HEAD_WIDTH:]).astype(jnp.bfloat16)
-            width = count * HEAD_WIDTH
-            columns = pl.ds(pl.multiple_of(first * HEAD_WIDTH, width), width)
-            out_ref[slot, :, columns] = jnp.concatenate(
-                [result[h * BALANCE_TOKENS : (h + 1) * BALANCE_TOKENS] for h in range(count)], axis=1
+            columns = pl.ds(pl.multiple_of(first * HEAD_WIDTH, TAIL_WIDTH), TAIL_WIDTH)
+            out_ref[slot, :, columns] = attend_pair(
+                slot_queries(slot, first, PAIR),
+                window[c, pl.ds(slot, MOST_BLK), 0].reshape(SPAN, HEAD_WIDTH),
+                window[c, pl.ds(slot, MOST_BLK), 1].reshape(SPAN, HEAD_WIDTH),
+                bias[slot, pl.ds(0, 1)],
+                diagonal,
             )
 
     def await_group(group, first, count):
@@ -378,7 +418,7 @@
 
         @pl.loop(0, GROUP // PAIR)
         def _(i):
-            attend(c, c * GROUP + i * PAIR, PAIR)
+            attend(c, c * GROUP + i * PAIR)
 
     await_halo(WHOLE)
 
@@ -388,19 +428,19 @@
 
         @pl.loop(0, HALF // PAIR)
         def _(j):
-            attend(WHOLE, WHOLE * GROUP + i * HALF + j * PAIR, PAIR)
+            attend(WHOLE, WHOLE * GROUP + i * HALF + j * PAIR)
 
     await_halo(LAST)
+    tail_window[...] = window[LAST]
 
     @pl.loop(0, PAIRS)
     def _(i):
         await_group(WHOLE + 2 + i, LAST * GROUP + i * PAIR, PAIR)
-        attend(LAST, LAST * GROUP + i * PAIR, PAIR)
-
-    @pl.loop(0, SINGLES)
-    def _(i):
-        await_group(GROUPS - SINGLES + i, QUERY_HEADS - SINGLES + i, 1)
-        attend(LAST, QUERY_HEADS - SINGLES + i, 1)
+        attend(LAST, LAST * GROUP + i * PAIR)
+
+    await_group(GROUPS - 1, TAIL, PAIR)
+    for slot in range(BLK_DEV):
+        tail_queries[slot] = slot_queries(slot, TAIL, PAIR)
 
     for piece in range(PIECES):
         for step in range(1, N_DP):
@@ -429,11 +469,17 @@
     width = QUERY_HEADS * HEAD_WIDTH
     smem = pl.BlockSpec(memory_space=pltpu.SMEM)
     anywhere = pl.BlockSpec(memory_space=pl.ANY)
-    attended = pl.pallas_call(
+    vmem = pl.BlockSpec(memory_space=pltpu.VMEM)
+    parts = pl.pallas_call(
         fused_kernel,
-        out_shape=pltpu.VMEM((*blocks, width), bf16),
+        out_shape=(
+            pltpu.VMEM((*blocks, width), bf16),
+            pltpu.VMEM((BLK_DEV, PAIR * tokens, HEAD_WIDTH), bf16),
+            pltpu.VMEM((WINDOW, 2, tokens, HEAD_WIDTH), bf16),
+            pltpu.VMEM((BLK_DEV, 8, HALO * tokens), jnp.float32),
+        ),
         in_specs=[anywhere, smem, anywhere, anywhere, anywhere],
-        out_specs=pl.BlockSpec(memory_space=pltpu.VMEM),
+        out_specs=(vmem, vmem, vmem, vmem),
         scratch_shapes=[
             pltpu.SMEM(block_source.shape[::-1], jnp.int32),
             pltpu.VMEM((*blocks, width), bf16),
@@ -444,7 +490,6 @@
             pltpu.VMEM((N_DP - 1, KEY_VALUE_HEADS, 2, tokens, HEAD_WIDTH), bf16),
             pltpu.VMEM((N_DP, KEY_VALUE_HEADS, 2, tokens, HEAD_WIDTH), bf16),
             pltpu.VMEM((KEY_VALUE_HEADS, WINDOW, 2, tokens, HEAD_WIDTH), bf16),
-            pltpu.VMEM((BLK_DEV, 8, HALO * tokens), jnp.float32),
             dma((1 + 2 * PIECES,)),
             dma((KEY_VALUE_HEADS,)),
             dma((GROUPS, N_DP - 1)),
@@ -466,6 +511,15 @@
         key_matrix.reshape(*blocks, kv_width),
         value_matrix.reshape(*blocks, kv_width),
     )
+    attended = pl.pallas_call(
+        finish_kernel,
+        out_shape=jax.ShapeDtypeStruct((*blocks, width), bf16),
+        in_specs=[vmem, vmem, vmem, vmem],
+        out_specs=anywhere,
+        scratch_shapes=[pltpu.VMEM((*blocks, TAIL_WIDTH), bf16), dma((BLK_DEV + 1,))],
+        compiler_params=pltpu.CompilerParams(vmem_limit_bytes=16 << 20),
+        name="finish_attention",
+    )(*parts)
     return attended.reshape(1, BLK_DEV * tokens, width)
 
 

time: 126 us -> 125 us (level)
  local copies, waits for them, and re-layouts: 3.4 us -> 0 us
  Pallas kernels: 122 us -> 124 us
    unnamed x1 -> x0, local copies, waits for them, and re-layouts: 3.4 us -> none
    pallas_call x1 -> x2, Pallas kernels: 122 us -> 124 us  [the longest x1 120 us: on_device(): pl.pallas_call(fused_kernel, out_shape=(pltpu.VMEM((*blocks, width), bf16...]
where the time goes in v5:
time: 125 us; the launch traced here: 124 us
  Pallas kernels  124 us (99%)
    pallas_call x1, Pallas kernels, on_device(): pl.pallas_call(fused_kernel, out_shape=(pltpu.VMEM((*blocks, width), bf16...  120 us
    pallas_call x1, Pallas kernels, on_device(): pl.pallas_call(finish_kernel, out_shape=jax.ShapeDtypeStruct((*blocks, wi...  3.38 us

profile of v5, /device:TPU:0, one launch (start us, length us, event | category | flops | bytes accessed | tf_op | source)
XLA Modules:
  0.0 123.6 jit_solution(8530597833777102501)
XLA Ops:
  0.0 120.2 %balanced_attention.1 = (bf16[4,128,8192]{2,1,0:T(8,128)(2,1)S(1)}, bf16[4,256,128]{2,1,0:T(8,128)(2,1)S(1)}, bf16[11,2,128,128]{3,2,1,0:T(8,128)(2,1)S(1)}, f32[4,8,896]{2,1,0:T(8,128)S(1)}) custom-call(s32[16,32]{1,0:T(8,128)} %bitcast.9, s32[128]{0:T(128)} %bitcast.10, bf16[4,128,8192]{2,1,0:T(8,128)(2,1)} %bitcast.6, bf16[4,128,1024]{2,1,0:T(8,128)(2,1)} %bitcast.7, ...), custom_call_target="tpu_custom_call" | custom-call | tf_op jit(solution)/shard_map/balanced_attention/pallas_call | solution.py:473
  120.2 3.4 %finish_attention.1 = bf16[4,128,8192]{2,1,0:T(8,128)(2,1)} custom-call(bf16[4,128,8192]{2,1,0:T(8,128)(2,1)S(1)} %get-tuple-element.9.ready_ref, bf16[4,256,128]{2,1,0:T(8,128)(2,1)S(1)} %get-tuple-element.10.queries_ref, bf16[11,2,128,128]{3,2,1,0:T(8,128)(2,1)S(1)} %get-tuple-element.11.window_ref, f32[4,8,896]{2,1,0:T(8,128)S(1)} %get-tuple-element.12.bias_ref), custom_call_target="tpu_custom_call" | custom-call | tf_op jit(solution)/shard_map/finish_attention/pallas_call | solution.py:514

commit v6 on v5

--- a/solution.py
+++ b/solution.py
@@ -15,23 +15,28 @@
 N_SP = 32
 GROUP = QUERY_HEADS // KEY_VALUE_HEADS
 PAIR = 2
+TWICE = 2
 WHOLE = KEY_VALUE_HEADS - 2
 HALF = GROUP // 2
 LAST = KEY_VALUE_HEADS - 1
 PAIRS = GROUP // PAIR - 1
-GROUPS = WHOLE + 2 + PAIRS + 1
+HEAD_GROUPS = WHOLE - TWICE
+GROUPS = HEAD_GROUPS + 2 + PAIRS + 1
 TAIL = QUERY_HEADS - PAIR
 TAIL_WIDTH = PAIR * HEAD_WIDTH
 READY_WIDTH = TAIL * HEAD_WIDTH
-PIECES = 2
-PIECE_HEADS = KEY_VALUE_HEADS // PIECES
-PIECE_WIDTH = PIECE_HEADS * HEAD_WIDTH
+PIECE_HEADS = (8,)
+PIECES = len(PIECE_HEADS)
 HALO = MOST_BLK - 1
 WINDOW = HALO + BLK_DEV
 SPAN = MOST_BLK * BALANCE_TOKENS
 MASKED = -1e30
 LOG2E = 1.4426950408889634
 MESH = pl.DeviceIdType.MESH
+
+
+def piece_range(piece):
+    return sum(PIECE_HEADS[:piece]), PIECE_HEADS[piece]
 
 
 def causal_levels():
@@ -60,16 +65,11 @@
 
 
 def finish_kernel(ready_ref, queries_ref, window_ref, bias_ref, out_hbm, staged, sem):
-    copies = [
-        pltpu.make_async_copy(
-            ready_ref.at[slot, :, pl.ds(0, READY_WIDTH)],
-            out_hbm.at[slot, :, pl.ds(0, READY_WIDTH)],
-            sem.at[slot],
-        )
-        for slot in range(BLK_DEV)
-    ]
-    for copy in copies:
-        copy.start()
+    columns = pl.ds(0, READY_WIDTH)
+    whole = pltpu.make_async_copy(
+        ready_ref.at[:, :, columns], out_hbm.at[:, :, columns], sem.at[0]
+    )
+    whole.start()
     diagonal = causal_levels()
     for slot in range(BLK_DEV):
         staged[slot] = attend_pair(
@@ -80,11 +80,10 @@
             diagonal,
         )
     last = pltpu.make_async_copy(
-        staged, out_hbm.at[:, :, pl.ds(READY_WIDTH, TAIL_WIDTH)], sem.at[BLK_DEV]
+        staged, out_hbm.at[:, :, pl.ds(READY_WIDTH, TAIL_WIDTH)], sem.at[1]
     )
     last.start()
-    for copy in copies:
-        copy.wait()
+    whole.wait()
     last.wait()
 
 
@@ -129,7 +128,8 @@
     source_load = pltpu.make_async_copy(source_hbm, source_ref, load_sem.at[0])
 
     def kv_load(kind, piece):
-        columns = pl.ds(piece * PIECE_WIDTH, PIECE_WIDTH)
+        first, count = piece_range(piece)
+        columns = pl.ds(first * HEAD_WIDTH, count * HEAD_WIDTH)
         return pltpu.make_async_copy(
             (k_hbm, v_hbm)[kind].at[:, :, columns],
             (k_local, v_local)[kind][piece],
@@ -222,7 +222,7 @@
         return step, jnp.where(step == 1, leaves[1], leaves[3])
 
     def kv_copy(piece, step):
-        heads = pl.ds(piece * PIECE_HEADS, PIECE_HEADS)
+        heads = pl.ds(*piece_range(piece))
         return pltpu.make_async_remote_copy(
             src_ref=kv_send.at[step - 1, heads],
             dst_ref=kv_recv.at[step, heads],
@@ -244,17 +244,21 @@
         )
 
     def each_group(act):
-        @pl.loop(0, WHOLE)
+        @pl.loop(0, TWICE)
+        def _(i):
+            act(i, i * 2 * GROUP, 2 * GROUP)
+
+        @pl.loop(2 * TWICE, WHOLE)
         def _(c):
-            act(c, c * GROUP, GROUP)
+            act(c - TWICE, c * GROUP, GROUP)
 
         @pl.loop(0, 2)
         def _(i):
-            act(WHOLE + i, WHOLE * GROUP + i * HALF, HALF)
+            act(HEAD_GROUPS + i, WHOLE * GROUP + i * HALF, HALF)
 
         @pl.loop(0, PAIRS + 1)
         def _(i):
-            act(WHOLE + 2 + i, LAST * GROUP + i * PAIR, PAIR)
+            act(HEAD_GROUPS + 2 + i, LAST * GROUP + i * PAIR, PAIR)
 
 
     def near_copy(c):
@@ -285,16 +289,17 @@
                 q_load(c).start()
         for turn in range(N_DP):
             step, leaf = turns(turn, piece)
-            for head in range(PIECE_HEADS):
+            first, count = piece_range(piece)
+            for head in range(count):
                 columns = pl.ds(head * HEAD_WIDTH, HEAD_WIDTH)
                 key = k_local[piece][leaf, :, columns]
                 value = v_local[piece][leaf, :, columns]
                 if turn < N_DP - 1:
-                    kv_send[step - 1, piece * PIECE_HEADS + head, 0] = key
-                    kv_send[step - 1, piece * PIECE_HEADS + head, 1] = value
+                    kv_send[step - 1, first + head, 0] = key
+                    kv_send[step - 1, first + head, 1] = value
                 else:
-                    kv_recv[0, piece * PIECE_HEADS + head, 0] = key
-                    kv_recv[0, piece * PIECE_HEADS + head, 1] = value
+                    kv_recv[0, first + head, 0] = key
+                    kv_recv[0, first + head, 1] = value
             if piece == 0 and turn == 0:
                 enter()
             if turn < N_DP - 1:
@@ -402,6 +407,10 @@
         for step in range(1, N_DP):
             q_copy(group, first, count, step).wait_recv()
 
+    def sent_group(group, first, count):
+        for step in range(1, N_DP):
+            q_copy(group, first, count, step).wait_send()
+
     def await_halo(c):
         @pl.when(s >= 1)
         def _():
@@ -411,20 +420,31 @@
         def _():
             far_copy(c).wait_recv()
 
-    @pl.loop(0, WHOLE)
-    def _(c):
+    def attend_whole(c):
         await_halo(c)
-        await_group(c, c * GROUP, GROUP)
 
         @pl.loop(0, GROUP // PAIR)
         def _(i):
             attend(c, c * GROUP + i * PAIR)
 
+    @pl.loop(0, TWICE)
+    def _(i):
+        await_group(i, i * 2 * GROUP, 2 * GROUP)
+
+        @pl.loop(0, 2)
+        def _(j):
+            attend_whole(2 * i + j)
+
+    @pl.loop(2 * TWICE, WHOLE)
+    def _(c):
+        await_group(c - TWICE, c * GROUP, GROUP)
+        attend_whole(c)
+
     await_halo(WHOLE)
 
     @pl.loop(0, 2)
     def _(i):
-        await_group(WHOLE + i, WHOLE * GROUP + i * HALF, HALF)
+        await_group(HEAD_GROUPS + i, WHOLE * GROUP + i * HALF, HALF)
 
         @pl.loop(0, HALF // PAIR)
         def _(j):
@@ -432,16 +452,6 @@
 
     await_halo(LAST)
     tail_window[...] = window[LAST]
-
-    @pl.loop(0, PAIRS)
-    def _(i):
-        await_group(WHOLE + 2 + i, LAST * GROUP + i * PAIR, PAIR)
-        attend(LAST, LAST * GROUP + i * PAIR)
-
-    await_group(GROUPS - 1, TAIL, PAIR)
-    for slot in range(BLK_DEV):
-        tail_queries[slot] = slot_queries(slot, TAIL, PAIR)
-
     for piece in range(PIECES):
         for step in range(1, N_DP):
             kv_copy(piece, step).wait_send()
@@ -453,11 +463,28 @@
         s < N_SP - 2,
     )
 
-    def sent_group(group, first, count):
-        for step in range(1, N_DP):
-            q_copy(group, first, count, step).wait_send()
-
-    each_group(sent_group)
+    @pl.loop(0, TWICE)
+    def _(i):
+        sent_group(i, i * 2 * GROUP, 2 * GROUP)
+
+    @pl.loop(2 * TWICE, WHOLE)
+    def _(c):
+        sent_group(c - TWICE, c * GROUP, GROUP)
+
+    @pl.loop(0, 2)
+    def _(i):
+        sent_group(HEAD_GROUPS + i, WHOLE * GROUP + i * HALF, HALF)
+
+    @pl.loop(0, PAIRS)
+    def _(i):
+        await_group(HEAD_GROUPS + 2 + i, LAST * GROUP + i * PAIR, PAIR)
+        attend(LAST, LAST * GROUP + i * PAIR)
+        sent_group(HEAD_GROUPS + 2 + i, LAST * GROUP + i * PAIR, PAIR)
+
+    await_group(GROUPS - 1, TAIL, PAIR)
+    for slot in range(BLK_DEV):
+        tail_queries[slot] = slot_queries(slot, TAIL, PAIR)
+    sent_group(GROUPS - 1, TAIL, PAIR)
 
 
 def on_device(query_matrix, key_matrix, value_matrix, block_source, documents):
@@ -483,8 +510,8 @@
         scratch_shapes=[
             pltpu.SMEM(block_source.shape[::-1], jnp.int32),
             pltpu.VMEM((*blocks, width), bf16),
-            [pltpu.VMEM((*blocks, PIECE_WIDTH), bf16)] * PIECES,
-            [pltpu.VMEM((*blocks, PIECE_WIDTH), bf16)] * PIECES,
+            [pltpu.VMEM((*blocks, count * HEAD_WIDTH), bf16) for count in PIECE_HEADS],
+            [pltpu.VMEM((*blocks, count * HEAD_WIDTH), bf16) for count in PIECE_HEADS],
             pltpu.VMEM((N_DP - 1, QUERY_HEADS, tokens, HEAD_WIDTH), bf16),
             pltpu.VMEM((N_DP, QUERY_HEADS, tokens, HEAD_WIDTH), bf16),
             pltpu.VMEM((N_DP - 1, KEY_VALUE_HEADS, 2, tokens, HEAD_WIDTH), bf16),
@@ -516,7 +543,7 @@
         out_shape=jax.ShapeDtypeStruct((*blocks, width), bf16),
         in_specs=[vmem, vmem, vmem, vmem],
         out_specs=anywhere,
-        scratch_shapes=[pltpu.VMEM((*blocks, TAIL_WIDTH), bf16), dma((BLK_DEV + 1,))],
+        scratch_shapes=[pltpu.VMEM((*blocks, TAIL_WIDTH), bf16), dma((2,))],
         compiler_params=pltpu.CompilerParams(vmem_limit_bytes=16 << 20),
         name="finish_attention",
     )(*parts)

time: 125 us -> 124 us (level)
  no operation moved by 1% of the time
where the time goes in v6:
time: 124 us
  Pallas kernels  124 us (100%)
    pallas_call x1, Pallas kernels, on_device(): pl.pallas_call(fused_kernel, out_shape=(pltpu.VMEM((*blocks, width), bf16...  120 us
    pallas_call x1, Pallas kernels, on_device(): pl.pallas_call(finish_kernel, out_shape=jax.ShapeDtypeStruct((*blocks, wi...  3.41 us

profile of v6, /device:TPU:0, one launch (start us, length us, event | category | flops | bytes accessed | tf_op | source)
XLA Modules:
  0.0 123.6 jit_solution(5609038814519257814)
XLA Ops:
  0.0 120.1 %balanced_attention.1 = (bf16[4,128,8192]{2,1,0:T(8,128)(2,1)S(1)}, bf16[4,256,128]{2,1,0:T(8,128)(2,1)S(1)}, bf16[11,2,128,128]{3,2,1,0:T(8,128)(2,1)S(1)}, f32[4,8,896]{2,1,0:T(8,128)S(1)}) custom-call(s32[16,32]{1,0:T(8,128)} %bitcast.9, s32[128]{0:T(128)} %bitcast.10, bf16[4,128,8192]{2,1,0:T(8,128)(2,1)} %bitcast.6, bf16[4,128,1024]{2,1,0:T(8,128)(2,1)} %bitcast.7, ...), custom_call_target="tpu_custom_call" | custom-call | tf_op jit(solution)/shard_map/balanced_attention/pallas_call | solution.py:500
  120.2 3.4 %finish_attention.1 = bf16[4,128,8192]{2,1,0:T(8,128)(2,1)} custom-call(bf16[4,128,8192]{2,1,0:T(8,128)(2,1)S(1)} %get-tuple-element.9.ready_ref, bf16[4,256,128]{2,1,0:T(8,128)(2,1)S(1)} %get-tuple-element.10.queries_ref, bf16[11,2,128,128]{3,2,1,0:T(8,128)(2,1)S(1)} %get-tuple-element.11.window_ref, f32[4,8,896]{2,1,0:T(8,128)S(1)} %get-tuple-element.12.bias_ref), custom_call_target="tpu_custom_call" | custom-call | tf_op jit(solution)/shard_map/finish_attention/pallas_call | solution.py:541

commit v7 on v6

--- a/solution.py
+++ b/solution.py
@@ -136,67 +136,67 @@
             load_sem.at[1 + 2 * piece + kind],
         )
 
+
+    def q_load(c):
+        columns = pl.ds(c * GROUP * HEAD_WIDTH, GROUP * HEAD_WIDTH)
+        return pltpu.make_async_copy(
+            q_hbm.at[:, :, columns], q_local.at[:, :, columns], q_load_sem.at[c]
+        )
+
+    barrier = pltpu.get_barrier_semaphore()
+    for step in range(1, N_DP):
+        pl.semaphore_signal(barrier, 1, device_id=dp_peer(step), device_id_type=MESH)
+
+    def greet(semaphore, column):
+        pl.semaphore_signal(semaphore, 1, device_id=(g, column), device_id_type=MESH)
+
+    @pl.when((s == 1) | (s >= 3))
+    def _():
+        greet(barrier, s - 1)
+
+    @pl.when(s >= 4)
+    def _():
+        greet(barrier, s - 2)
+
+    def enter():
+        @pl.when(s == 0)
+        def _():
+            pl.semaphore_wait(barrier, 4)
+            greet(barrier, 2)
+
+        @pl.when(s == 1)
+        def _():
+            pl.semaphore_wait(barrier, 3)
+            greet(barrier, 2)
+            greet(barrier, 3)
+
+        @pl.when(s == 2)
+        def _():
+            pl.semaphore_wait(barrier, 7)
+            greet(ready, 0)
+            greet(ready, 1)
+
+        @pl.when(s == 3)
+        def _():
+            pl.semaphore_wait(barrier, 6)
+            greet(ready, 1)
+
+        @pl.when((s >= 4) & (s <= N_SP - 3))
+        def _():
+            pl.semaphore_wait(barrier, 5)
+
+        @pl.when(s == N_SP - 2)
+        def _():
+            pl.semaphore_wait(barrier, 4)
+
+        @pl.when(s == N_SP - 1)
+        def _():
+            pl.semaphore_wait(barrier, 3)
+
     source_load.start()
     for piece in range(PIECES):
         kv_load(0, piece).start()
         kv_load(1, piece).start()
-
-    def q_load(c):
-        columns = pl.ds(c * GROUP * HEAD_WIDTH, GROUP * HEAD_WIDTH)
-        return pltpu.make_async_copy(
-            q_hbm.at[:, :, columns], q_local.at[:, :, columns], q_load_sem.at[c]
-        )
-
-    barrier = pltpu.get_barrier_semaphore()
-    for step in range(1, N_DP):
-        pl.semaphore_signal(barrier, 1, device_id=dp_peer(step), device_id_type=MESH)
-
-    def greet(semaphore, column):
-        pl.semaphore_signal(semaphore, 1, device_id=(g, column), device_id_type=MESH)
-
-    @pl.when((s == 1) | (s >= 3))
-    def _():
-        greet(barrier, s - 1)
-
-    @pl.when(s >= 4)
-    def _():
-        greet(barrier, s - 2)
-
-    def enter():
-        @pl.when(s == 0)
-        def _():
-            pl.semaphore_wait(barrier, 4)
-            greet(barrier, 2)
-
-        @pl.when(s == 1)
-        def _():
-            pl.semaphore_wait(barrier, 3)
-            greet(barrier, 2)
-            greet(barrier, 3)
-
-        @pl.when(s == 2)
-        def _():
-            pl.semaphore_wait(barrier, 7)
-            greet(ready, 0)
-            greet(ready, 1)
-
-        @pl.when(s == 3)
-        def _():
-            pl.semaphore_wait(barrier, 6)
-            greet(ready, 1)
-
-        @pl.when((s >= 4) & (s <= N_SP - 3))
-        def _():
-            pl.semaphore_wait(barrier, 5)
-
-        @pl.when(s == N_SP - 2)
-        def _():
-            pl.semaphore_wait(barrier, 4)
-
-        @pl.when(s == N_SP - 1)
-        def _():
-            pl.semaphore_wait(barrier, 3)
-
     source_load.wait()
 
     def departing(step):

time: 124 us -> 124 us (level)
  no operation moved by 1% of the time
where the time goes in v7:
time: 124 us
  Pallas kernels  124 us (100%)
    pallas_call x1, Pallas kernels, on_device(): pl.pallas_call(fused_kernel, out_shape=(pltpu.VMEM((*blocks, width), bf16...  120 us
    pallas_call x1, Pallas kernels, on_device(): pl.pallas_call(finish_kernel, out_shape=jax.ShapeDtypeStruct((*blocks, wi...  3.41 us

profile of v7, /device:TPU:0, one launch (start us, length us, event | category | flops | bytes accessed | tf_op | source)
XLA Modules:
  0.0 123.6 jit_solution(3622803503220744530)
XLA Ops:
  0.0 120.2 %balanced_attention.1 = (bf16[4,128,8192]{2,1,0:T(8,128)(2,1)S(1)}, bf16[4,256,128]{2,1,0:T(8,128)(2,1)S(1)}, bf16[11,2,128,128]{3,2,1,0:T(8,128)(2,1)S(1)}, f32[4,8,896]{2,1,0:T(8,128)S(1)}) custom-call(s32[16,32]{1,0:T(8,128)} %bitcast.9, s32[128]{0:T(128)} %bitcast.10, bf16[4,128,8192]{2,1,0:T(8,128)(2,1)} %bitcast.6, bf16[4,128,1024]{2,1,0:T(8,128)(2,1)} %bitcast.7, ...), custom_call_target="tpu_custom_call" | custom-call | tf_op jit(solution)/shard_map/balanced_attention/pallas_call | solution.py:500
  120.2 3.4 %finish_attention.1 = bf16[4,128,8192]{2,1,0:T(8,128)(2,1)} custom-call(bf16[4,128,8192]{2,1,0:T(8,128)(2,1)S(1)} %get-tuple-element.9.ready_ref, bf16[4,256,128]{2,1,0:T(8,128)(2,1)S(1)} %get-tuple-element.10.queries_ref, bf16[11,2,128,128]{3,2,1,0:T(8,128)(2,1)S(1)} %get-tuple-element.11.window_ref, f32[4,8,896]{2,1,0:T(8,128)S(1)} %get-tuple-element.12.bias_ref), custom_call_target="tpu_custom_call" | custom-call | tf_op jit(solution)/shard_map/finish_attention/pallas_call | solution.py:541
